TPU v7x, 128 devices: a whole 4x4x4 slice. The times are simulated.
128 devices in a mesh: layer: 4 (over x), head: 32 (over y, z, core).
Axes of the slice: x: 4, y: 4, z: 4, core: 2. Of those that a mesh axis runs over, the one named last changes fastest.
Arguments:
- momentum: bfloat16 [4, 32768, 512], P(None, ('layer', 'head')), may hold values from -6 to 6
- grad_one: bfloat16 [4, 32768, 512], P(None, ('layer', 'head')), may hold values from -6 to 6
- grad_two: bfloat16 [4, 32768, 512], P(None, ('layer', 'head')), may hold values from -60 to 60
Outputs:
- update_one: float32 [4, 32768, 512], P(None, ('layer', 'head'))
- update_two: float32 [4, 32768, 512], P(None, ('layer', 'head'))
All inputs are finite; a program needn't handle non-finite values.
Results may differ from a plain program's by a relative error of at most 0.0065.
Values may be sent and summed in bfloat16 or wider, within the bound.
A program may use at most 64 MiB of HBM per device.

v0:
```python
import math

import jax
import jax.numpy as jnp
from jax import lax
from jax.sharding import Mesh
from jax.sharding import PartitionSpec as P

HEAD_ROWS = 256
NS_ITERS = 5
ROWS = 32768
HEAD = ("head_0", "head_1", "head_2")
LAYER_HEAD = ("layer", "head_0", "head_1", "head_2")


quintic_a = 3.4445
quintic_b = -4.775
quintic_c = 2.0315
norm_epsilon = 1e-07
momentum_decay = 0.95


def copy_for_each(x, axis):
    copies = jnp.broadcast_to(x, (lax.axis_size(axis), *x.shape))
    return lax.all_to_all(copies, axis, split_axis=0, concat_axis=0, tiled=True)


def over_copies(x, axis):
    return copy_for_each(x, axis).sum(axis=0)


def padded_to(lines, length):
    spare = -len(lines) % length
    return jnp.pad(lines, [(0, spare)] + [(0, 0)] * (lines.ndim - 1))


def in_order(tiles, dim):
    tiles = jnp.moveaxis(tiles, 0, dim)
    shape = tiles.shape
    return tiles.reshape(*shape[:dim], shape[dim] * shape[dim + 1], *shape[dim + 2 :])


def whole_of(x, axes, dim):
    far, near = axes
    tiles = copy_for_each(copy_for_each(x, far), near)
    return in_order(tiles.swapaxes(0, 1).reshape(-1, *x.shape), dim)


def in_blocks(x, dim, length):
    before, after = (x.shape[:dim], x.shape[dim + 1 :])
    return jnp.moveaxis(x.reshape(*before, length, -1, *after), dim, 0)


def sent_and_summed(x, axis, dim):
    tiles = in_blocks(x, dim, lax.axis_size(axis))
    arrived = lax.all_to_all(tiles, axis, split_axis=0, concat_axis=0, tiled=True)
    return arrived.sum(axis=0)


def sum_in_two_steps(x, axes, dim):
    far, near = axes
    own = sent_and_summed(in_blocks(x, dim, lax.axis_size(far)), near, dim + 1)
    return jnp.sum(lax.all_to_all(own, far, 0, 0, tiled=True), axis=0)


def sum_by_parts(x, axes):
    lines = x.reshape(-1, x.shape[-1])
    padded = padded_to(lines, lax.axis_size(axes[0]) * lax.axis_size(axes[1]))
    whole = whole_of(sum_in_two_steps(padded, axes, 0), axes, 0)
    return lax.slice_in_dim(whole, 0, len(lines)).reshape(x.shape)


def block_newton(blocks):
    wide = blocks.astype(jnp.float32)
    squares = jnp.sum(jnp.square(wide), axis=(1, 2), keepdims=True)
    current = wide / (jnp.sqrt(squares) + norm_epsilon)
    for iteration in range(NS_ITERS):
        gram_part = jnp.einsum("nrl,nsl->nrs", current, current, precision=lax.Precision.HIGHEST)
        polynomial = quintic_b * gram_part + quintic_c * jnp.einsum(
            "nrs,nst->nrt", gram_part, gram_part, precision=lax.Precision.HIGHEST
        )
        current = quintic_a * current + jnp.einsum(
            "nrs,nsl->nrl", polynomial, current, precision=lax.Precision.HIGHEST
        )
    return current


def shards(momentum, grad_one, grad_two):
    latent = momentum.shape[-1]
    momentum_one = (
        momentum_decay * momentum.astype(jnp.float32) + grad_one.astype(jnp.float32)
    ).astype(jnp.bfloat16)
    momentum_two = (
        momentum_decay * momentum_one.astype(jnp.float32) + grad_two.astype(jnp.float32)
    ).astype(jnp.bfloat16)
    team_rows = lax.all_to_all(momentum_two, "layer", split_axis=0, concat_axis=1, tiled=True)[0]
    update_one = block_newton(momentum_one) * math.sqrt(max(HEAD_ROWS, latent))
    team_wide = team_rows.astype(jnp.float32)
    local_squares = jnp.sum(jnp.square(team_wide))
    norm_squared = over_copies(local_squares, HEAD)
    current = team_wide / (jnp.sqrt(norm_squared) + norm_epsilon)
    for iteration in range(NS_ITERS):
        gram_part = jnp.einsum("rk,rl->kl", current, current, precision=lax.Precision.HIGHEST)
        gram_total = sum_by_parts(gram_part, (("head_0", "head_1"), "head_2"))
        polynomial = quintic_b * gram_total + quintic_c * jnp.dot(
            gram_total, gram_total, precision=lax.Precision.HIGHEST
        )
        current = quintic_a * current + jnp.dot(
            current, polynomial, precision=lax.Precision.HIGHEST
        )
    scaled = (current * math.sqrt(ROWS))[None]
    update_two = lax.all_to_all(scaled, "layer", split_axis=1, concat_axis=0, tiled=True)
    return (update_one, update_two)


def solution(mesh):
    split = Mesh(
        mesh.devices.reshape(mesh.shape["layer"], 4, 4, 2), ("layer", "head_0", "head_1", "head_2")
    )
    return jax.shard_map(
        shards,
        mesh=split,
        in_specs=(P(None, LAYER_HEAD, None), P(None, LAYER_HEAD, None), P(None, LAYER_HEAD, None)),
        out_specs=(P(None, LAYER_HEAD, None), P(None, LAYER_HEAD, None)),
        check_vma=False,
    )
```

profile of v0, /device:TPU:1, one launch (start us, length us, event | category | flops | bytes accessed | tf_op | source)
XLA Modules:
  0.0 339.9 jit_solution(18047398278646834772)
XLA Ops:
  4.1 18.9 %all_to_all.127 = bf16[4,256,512]{2,1,0:T(8,128)(2,1)S(1)} all-to-all(bf16[4,256,512]{2,1,0:T(8,128)(2,1)S(1)} %get-tuple-element.2), channel_id=1, replica_groups=mesh['layer'=4,'head_0'=4,'head_1'=4,'head_2'=2] {'layer'}, dimensions={0} | all-to-all | bytes 2097152 | tf_op jit(solution)/shard_map/all_to_all | solution.py:96
  24.7 16.7 %all_to_all.128 = f32[32,1,1]{2,1,0:T(1,128)S(1)} all-to-all(f32[32,1,1]{2,1,0:T(1,128)S(1)} %broadcast_in_dim.37), channel_id=1, replica_groups=mesh['layer'=4,'head_0'=4,'head_1'=4,'head_2'=2] {'head_0','head_1','hea..., dimensions={0} | all-to-all | bytes 256 | tf_op jit(solution)/shard_map/all_to_all | solution.py:25
  45.1 5.1 %convolution_bitcast_fusion = f32[2,16,16,512]{3,2,0,1:T(8,128)S(1)} fusion(f32[16,2,16,1024]{3,2,1,0:T(8,128)} %bitcast.105, f32[1024,512,1,1]{1,0,3,2:T(8,128)S(1)} %bitcast.98), kind=kOutput, calls=%fused_computation.31 | convolution fusion | flops 3221225472 | bytes 5242880 | tf_op jit(solution)/shard_map/rk,rl->kl/dot_general | solution.py:103
  50.3 4.9 %all_to_all.129 = f32[2,16,16,512]{3,2,1,0:T(8,128)S(1)} all-to-all(f32[2,16,16,512]{3,2,1,0:T(8,128)S(1)} %copy.33), channel_id=1, replica_groups=mesh['layer'=4,'head_0'=4,'head_1'=4,'head_2'=2] {'head_2'}, dimensions={0} | all-to-all | bytes 2097152 | tf_op jit(solution)/shard_map/all_to_all | solution.py:56
  55.2 13.1 %all_to_all.130 = f32[16,16,512]{2,1,0:T(8,128)S(1)} all-to-all(f32[16,16,512]{2,1,0:T(8,128)S(1)} %reduce_sum.120), channel_id=1, replica_groups=mesh['layer'=4,'head_0'=4,'head_1'=4,'head_2'=2] {'head_0','head_1'}, dimensions={0} | all-to-all | bytes 1048576 | tf_op jit(solution)/shard_map/all_to_all | solution.py:63
  68.5 12.7 %all_to_all.131 = f32[16,16,512]{2,1,0:T(8,128)S(1)} all-to-all(f32[16,16,512]{2,1,0:T(8,128)S(1)} %broadcast_in_dim.38), channel_id=1, replica_groups=mesh['layer'=4,'head_0'=4,'head_1'=4,'head_2'=2] {'head_0','head_1'}, dimensions={0} | all-to-all | bytes 1048576 | tf_op jit(solution)/shard_map/all_to_all | solution.py:25
  81.3 7.7 %all_to_all.132 = f32[2,16,16,512]{3,2,1,0:T(8,128)S(1)} all-to-all(f32[2,16,16,512]{3,2,1,0:T(8,128)S(1)} %broadcast_in_dim.39), channel_id=1, replica_groups=mesh['layer'=4,'head_0'=4,'head_1'=4,'head_2'=2] {'head_2'}, dimensions={0} | all-to-all | bytes 2097152 | tf_op jit(solution)/shard_map/all_to_all | solution.py:25
  98.2 4.6 %all_to_all.133 = f32[2,16,16,512]{3,2,1,0:T(8,128)S(1)} all-to-all(f32[2,16,16,512]{3,2,1,0:T(8,128)S(1)} %bitcast.110), channel_id=1, replica_groups=mesh['layer'=4,'head_0'=4,'head_1'=4,'head_2'=2] {'head_2'}, dimensions={0} | all-to-all | bytes 2097152 | tf_op jit(solution)/shard_map/all_to_all | solution.py:56
  103.7 13.7 %all_to_all.134 = f32[16,16,512]{2,1,0:T(8,128)S(1)} all-to-all(f32[16,16,512]{2,1,0:T(8,128)} %reduce_sum.122), channel_id=1, replica_groups=mesh['layer'=4,'head_0'=4,'head_1'=4,'head_2'=2] {'head_0','head_1'}, dimensions={0} | all-to-all | bytes 1048576 | tf_op jit(solution)/shard_map/all_to_all | solution.py:63
  117.5 13.0 %all_to_all.135 = f32[16,16,512]{2,1,0:T(8,128)S(1)} all-to-all(f32[16,16,512]{2,1,0:T(8,128)S(1)} %broadcast_in_dim.40), channel_id=1, replica_groups=mesh['layer'=4,'head_0'=4,'head_1'=4,'head_2'=2] {'head_0','head_1'}, dimensions={0} | all-to-all | bytes 1048576 | tf_op jit(solution)/shard_map/all_to_all | solution.py:25
  130.6 8.2 %all_to_all.136 = f32[2,16,16,512]{3,2,1,0:T(8,128)S(1)} all-to-all(f32[2,16,16,512]{3,2,1,0:T(8,128)S(1)} %broadcast_in_dim.41), channel_id=1, replica_groups=mesh['layer'=4,'head_0'=4,'head_1'=4,'head_2'=2] {'head_2'}, dimensions={0} | all-to-all | bytes 2097152 | tf_op jit(solution)/shard_map/all_to_all | solution.py:25
  144.3 3.7 %fusion.22 = f32[512,512]{1,0:T(8,128)S(1)} fusion(f32[1024,512]{1,0:T(8,128)S(1)} %multiply_add_fusion.2), kind=kOutput, calls=%fused_computation.54 | convolution fusion | flops 3221225472 | bytes 3145728 | tf_op jit(solution)/shard_map/rk,rl->kl/dot_general | solution.py:103
  148.1 4.7 %all_to_all.137 = f32[2,16,16,512]{3,2,1,0:T(8,128)S(1)} all-to-all(f32[2,16,16,512]{3,2,1,0:T(8,128)S(1)} %bitcast.112), channel_id=1, replica_groups=mesh['layer'=4,'head_0'=4,'head_1'=4,'head_2'=2] {'head_2'}, dimensions={0} | all-to-all | bytes 2097152 | tf_op jit(solution)/shard_map/all_to_all | solution.py:56
  157.7 9.8 %all-to-all-done.11 = f32[16,16,512]{2,1,0:T(8,128)S(1)} async-done(((f32[16,16,512]{2,1,0:T(8,128)}), f32[16,16,512]{2,1,0:T(8,128)S(1)}, u32[]{:S(2)}, u32[]{:S(2)}) %all-to-all-start.11) | async-done | bytes 524320 | tf_op jit(solution)/shard_map/all_to_all | solution.py:63
  168.4 4.4 %all-to-all-start.12 = ((f32[16,16,512]{2,1,0:T(8,128)}), f32[16,16,512]{2,1,0:T(8,128)S(1)}, u32[]{:S(2)}, u32[]{:S(2)}) async-start(f32[16,16,512]{2,1,0:T(8,128)} %broadcast_in_dim.42), calls=%async_computation.12 | async-start | bytes 1048576 | tf_op jit(solution)/shard_map/all_to_all | solution.py:25
  177.4 4.2 %all-to-all-done.12 = f32[16,16,512]{2,1,0:T(8,128)S(1)} async-done(((f32[16,16,512]{2,1,0:T(8,128)}), f32[16,16,512]{2,1,0:T(8,128)S(1)}, u32[]{:S(2)}, u32[]{:S(2)}) %all-to-all-start.12) | async-done | bytes 524320 | tf_op jit(solution)/shard_map/all_to_all | solution.py:25
  181.7 7.8 %all_to_all.138 = f32[2,16,16,512]{3,2,1,0:T(8,128)S(1)} all-to-all(f32[2,16,16,512]{3,2,1,0:T(8,128)S(1)} %broadcast_in_dim.43), channel_id=1, replica_groups=mesh['layer'=4,'head_0'=4,'head_1'=4,'head_2'=2] {'head_2'}, dimensions={0} | all-to-all | bytes 2097152 | tf_op jit(solution)/shard_map/all_to_all | solution.py:25
  198.7 5.4 %all_to_all.139 = f32[2,16,16,512]{3,2,1,0:T(8,128)} all-to-all(f32[2,16,16,512]{3,2,1,0:T(8,128)S(1)} %bitcast.114), channel_id=1, replica_groups=mesh['layer'=4,'head_0'=4,'head_1'=4,'head_2'=2] {'head_2'}, dimensions={0} | all-to-all | bytes 2097152 | tf_op jit(solution)/shard_map/all_to_all | solution.py:56
  206.2 4.4 %all-to-all-start.15 = ((f32[16,16,512]{2,1,0:T(8,128)}), f32[16,16,512]{2,1,0:T(8,128)}, u32[]{:S(2)}, u32[]{:S(2)}) async-start(f32[16,16,512]{2,1,0:T(8,128)} %reduce_sum.126), calls=%async_computation.15 | async-start | bytes 1048576 | tf_op jit(solution)/shard_map/all_to_all | solution.py:63
  210.7 3.6 %multiply_add_fusion.7 = f32[4,256,512]{2,1,0:T(8,128)S(1)} fusion(f32[4,256,256]{2,1,0:T(8,128)} %fusion.14, bf16[4,256,512]{2,1,0:T(8,128)(2,1)S(1)} %copy-done.11, f32[4]{0:T(128)S(1)} %sqrt_add_fusion), kind=kOutput, calls=%fused_computation.18 | convolution fusion | flops 1613758464 | bytes 4194320 | tf_op jit(solution)/shard_map/nrs,nsl->nrl/dot_general | solution.py:82
  222.8 4.3 %all-to-all-start.16 = ((f32[16,16,512]{2,1,0:T(8,128)}), f32[16,16,512]{2,1,0:T(8,128)}, u32[]{:S(2)}, u32[]{:S(2)}) async-start(f32[16,16,512]{2,1,0:T(8,128)} %broadcast_in_dim.44), calls=%async_computation.16 | async-start | bytes 1048576 | tf_op jit(solution)/shard_map/all_to_all | solution.py:25
  232.0 4.3 %all-to-all-done.16 = f32[16,16,512]{2,1,0:T(8,128)} async-done(((f32[16,16,512]{2,1,0:T(8,128)}), f32[16,16,512]{2,1,0:T(8,128)}, u32[]{:S(2)}, u32[]{:S(2)}) %all-to-all-start.16) | async-done | bytes 524320 | tf_op jit(solution)/shard_map/all_to_all | solution.py:25
  237.5 7.8 %all_to_all.140 = f32[2,16,16,512]{3,2,1,0:T(8,128)S(1)} all-to-all(f32[2,16,16,512]{3,2,1,0:T(8,128)S(1)} %broadcast_in_dim.45), channel_id=1, replica_groups=mesh['layer'=4,'head_0'=4,'head_1'=4,'head_2'=2] {'head_2'}, dimensions={0} | all-to-all | bytes 2097152 | tf_op jit(solution)/shard_map/all_to_all | solution.py:25
  250.8 3.7 %fusion.24 = f32[512,512]{1,0:T(8,128)S(1)} fusion(f32[1024,512]{1,0:T(8,128)S(1)} %multiply_add_fusion), kind=kOutput, calls=%fused_computation.56 | convolution fusion | flops 3221225472 | bytes 3145728 | tf_op jit(solution)/shard_map/rk,rl->kl/dot_general | solution.py:103
  254.6 4.7 %all_to_all.141 = f32[2,16,16,512]{3,2,1,0:T(8,128)S(1)} all-to-all(f32[2,16,16,512]{3,2,1,0:T(8,128)S(1)} %bitcast.116), channel_id=1, replica_groups=mesh['layer'=4,'head_0'=4,'head_1'=4,'head_2'=2] {'head_2'}, dimensions={0} | all-to-all | bytes 2097152 | tf_op jit(solution)/shard_map/all_to_all | solution.py:56
  260.2 4.4 %all-to-all-start.19 = ((f32[16,16,512]{2,1,0:T(8,128)}), f32[16,16,512]{2,1,0:T(8,128)}, u32[]{:S(2)}, u32[]{:S(2)}) async-start(f32[16,16,512]{2,1,0:T(8,128)} %reduce_sum.128), calls=%async_computation.19 | async-start | bytes 1048576 | tf_op jit(solution)/shard_map/all_to_all | solution.py:63
  268.1 6.8 %all-to-all-done.19 = f32[16,16,512]{2,1,0:T(8,128)} async-done(((f32[16,16,512]{2,1,0:T(8,128)}), f32[16,16,512]{2,1,0:T(8,128)}, u32[]{:S(2)}, u32[]{:S(2)}) %all-to-all-start.19) | async-done | bytes 524320 | tf_op jit(solution)/shard_map/all_to_all | solution.py:63
  276.8 4.3 %all-to-all-start.20 = ((f32[16,16,512]{2,1,0:T(8,128)}), f32[16,16,512]{2,1,0:T(8,128)}, u32[]{:S(2)}, u32[]{:S(2)}) async-start(f32[16,16,512]{2,1,0:T(8,128)} %broadcast_in_dim.46), calls=%async_computation.20 | async-start | bytes 1048576 | tf_op jit(solution)/shard_map/all_to_all | solution.py:25
  286.6 3.7 %all-to-all-done.20 = f32[16,16,512]{2,1,0:T(8,128)} async-done(((f32[16,16,512]{2,1,0:T(8,128)}), f32[16,16,512]{2,1,0:T(8,128)}, u32[]{:S(2)}, u32[]{:S(2)}) %all-to-all-start.20) | async-done | bytes 524320 | tf_op jit(solution)/shard_map/all_to_all | solution.py:25
  291.5 7.6 %all_to_all.142 = f32[2,16,16,512]{3,2,1,0:T(8,128)S(1)} all-to-all(f32[2,16,16,512]{3,2,1,0:T(8,128)S(1)} %broadcast_in_dim.47), channel_id=1, replica_groups=mesh['layer'=4,'head_0'=4,'head_1'=4,'head_2'=2] {'head_2'}, dimensions={0} | all-to-all | bytes 2097152 | tf_op jit(solution)/shard_map/all_to_all | solution.py:25
  308.3 3.9 %all-to-all-start.22 = ((f32[1,1024,512]{2,0,1:T(1,128)}), f32[1,1024,512]{2,0,1:T(1,128)S(1)}, u32[]{:S(2)}, u32[]{:S(2)}) async-start(f32[1,1024,512]{2,0,1:T(1,128)} %copy.43), calls=%async_computation.22 | async-start | bytes 4194304 | tf_op jit(solution)/shard_map/all_to_all | solution.py:112
  322.8 15.4 %all-to-all-done.22 = f32[1,1024,512]{2,0,1:T(1,128)S(1)} async-done(((f32[1,1024,512]{2,0,1:T(1,128)}), f32[1,1024,512]{2,0,1:T(1,128)S(1)}, u32[]{:S(2)}, u32[]{:S(2)}) %all-to-all-start.22) | async-done | bytes 2097184 | tf_op jit(solution)/shard_map/all_to_all | solution.py:112
  (92 shorter events, 100.5 us)
Async XLA Ops:
  43.0 2.0 copy-start.7
  89.1 1.9 copy-start.8
  144.3 3.7 %copy-start.2 = (f32[1024,512]{1,0:T(8,128)}, f32[1024,512]{1,0:T(8,128)S(1)}, u32[]{:S(2)}) copy-start(f32[1024,512]{1,0:T(8,128)S(1)} %multiply_add_fusion.2) | copy-start | bytes 6291460
  148.1 9.2 %copy-start.11 = (bf16[4,256,512]{2,1,0:T(8,128)(2,1)S(1)}, bf16[4,256,512]{2,1,0:T(8,128)(2,1)}, u32[]{:S(2)}) copy-start(bf16[4,256,512]{2,1,0:T(8,128)(2,1)} %get-tuple-element.3) | copy-start | bytes 3145732
  153.7 13.7 %all-to-all-start.11 = ((f32[16,16,512]{2,1,0:T(8,128)}), f32[16,16,512]{2,1,0:T(8,128)S(1)}, u32[]{:S(2)}, u32[]{:S(2)}) async-start(f32[16,16,512]{2,1,0:T(8,128)} %reduce_sum.124), calls=%async_computation.11 | async-start | bytes 1048576 | tf_op jit(solution)/shard_map/all_to_all | solution.py:63
  168.4 13.2 %all-to-all-start.12 = ((f32[16,16,512]{2,1,0:T(8,128)}), f32[16,16,512]{2,1,0:T(8,128)S(1)}, u32[]{:S(2)}, u32[]{:S(2)}) async-start(f32[16,16,512]{2,1,0:T(8,128)} %broadcast_in_dim.42), calls=%async_computation.12 | async-start | bytes 1048576 | tf_op jit(solution)/shard_map/all_to_all | solution.py:25
  189.6 1.9 copy-start.3
  206.2 14.6 %all-to-all-start.15 = ((f32[16,16,512]{2,1,0:T(8,128)}), f32[16,16,512]{2,1,0:T(8,128)}, u32[]{:S(2)}, u32[]{:S(2)}) async-start(f32[16,16,512]{2,1,0:T(8,128)} %reduce_sum.126), calls=%async_computation.15 | async-start | bytes 1048576 | tf_op jit(solution)/shard_map/all_to_all | solution.py:63
  214.3 1.3 copy-start.9
  222.8 13.5 %all-to-all-start.16 = ((f32[16,16,512]{2,1,0:T(8,128)}), f32[16,16,512]{2,1,0:T(8,128)}, u32[]{:S(2)}, u32[]{:S(2)}) async-start(f32[16,16,512]{2,1,0:T(8,128)} %broadcast_in_dim.44), calls=%async_computation.16 | async-start | bytes 1048576 | tf_op jit(solution)/shard_map/all_to_all | solution.py:25
  227.0 1.6 copy-start.10
  250.8 3.7 %copy-start = (f32[1024,512]{1,0:T(8,128)}, f32[1024,512]{1,0:T(8,128)S(1)}, u32[]{:S(2)}) copy-start(f32[1024,512]{1,0:T(8,128)S(1)} %multiply_add_fusion) | copy-start | bytes 6291460
  254.6 10.1 %copy-start.4 = (f32[4,256,512]{2,1,0:T(8,128)S(1)}, f32[4,256,512]{2,1,0:T(8,128)}, u32[]{:S(2)}) copy-start(f32[4,256,512]{2,1,0:T(8,128)} %multiply_add_fusion.6) | copy-start | bytes 6291460
  260.2 14.6 %all-to-all-start.19 = ((f32[16,16,512]{2,1,0:T(8,128)}), f32[16,16,512]{2,1,0:T(8,128)}, u32[]{:S(2)}, u32[]{:S(2)}) async-start(f32[16,16,512]{2,1,0:T(8,128)} %reduce_sum.128), calls=%async_computation.19 | async-start | bytes 1048576 | tf_op jit(solution)/shard_map/all_to_all | solution.py:63
  276.8 13.5 %all-to-all-start.20 = ((f32[16,16,512]{2,1,0:T(8,128)}), f32[16,16,512]{2,1,0:T(8,128)}, u32[]{:S(2)}, u32[]{:S(2)}) async-start(f32[16,16,512]{2,1,0:T(8,128)} %broadcast_in_dim.46), calls=%async_computation.20 | async-start | bytes 1048576 | tf_op jit(solution)/shard_map/all_to_all | solution.py:25
  283.2 1.3 copy-start.5
  299.2 1.9 copy-start.1
  308.3 29.9 %all-to-all-start.22 = ((f32[1,1024,512]{2,0,1:T(1,128)}), f32[1,1024,512]{2,0,1:T(1,128)S(1)}, u32[]{:S(2)}, u32[]{:S(2)}) async-start(f32[1,1024,512]{2,0,1:T(1,128)} %copy.43), calls=%async_computation.22 | async-start | bytes 4194304 | tf_op jit(solution)/shard_map/all_to_all | solution.py:112
  312.1 1.6 copy-start.6
where the time goes:
time: 346 us; the launch traced here: 340 us
  blocking collectives  151 us (44%)
  matrix products  79.5 us (23%)
  waiting for transfers between devices  47.2 us (14%)
  starting transfers between devices  29.2 us (8%)
  local copies, waits for them, and re-layouts  17.2 us (5%)
  other arithmetic  13.1 us (4%)
    all_to_all x8, blocking collectives, copy_for_each(): return lax.all_to_all(copies, axis, split_axis=0, concat_axis=0, tiled=True)  81.6 us
    all_to_all x2, blocking collectives, sum_in_two_steps(): return jnp.sum(lax.all_to_all(own, far, 0, 0, tiled=True), axis=0)  26.8 us
    all_to_all x5, blocking collectives, sent_and_summed(): lax.all_to_all(tiles, axis, split_axis=0, concat_axis=0, tiled=True)  24.2 us
    all_to_all x3, waiting for transfers between devices, sum_in_two_steps(): return jnp.sum(lax.all_to_all(own, far, 0, 0, tiled=True), axis=0)  19.7 us
    dot_general x5, matrix products, shards(): jnp.einsum('rk,rl->kl', current, current, precision=lax.Precision.HIGHEST)  19.4 us
    all_to_all x1, blocking collectives, shards(): lax.all_to_all(momentum_two, 'layer', split_axis=0, concat_axis=1, tiled=...  18.9 us
    dot_general x5, matrix products, shards(): jnp.dot(current, polynomial, precision=lax.Precision.HIGHEST)  17.7 us
    all_to_all x1, waiting for transfers between devices, shards(): lax.all_to_all(scaled, 'layer', split_axis=1, concat_axis=0, tiled=True)  15.4 us
  transfers between devices with their start and end apart: 7, of which 7 were waited for; matrix products, arithmetic and copies ran while one was open for 10% of the time, Pallas kernels for 0%

commit v1 on v0

v1 whole, which is shorter than its diff:
```python
import math

import jax
import jax.numpy as jnp
from jax import lax
from jax.sharding import PartitionSpec as P

HEAD_ROWS = 256
NS_ITERS = 5
ROWS = 32768

quintic_a = 3.4445
quintic_b = -4.775
quintic_c = 2.0315
norm_epsilon = 1e-07
momentum_decay = 0.95
PREC = lax.Precision.HIGH


def mm(a, b):
    return jnp.matmul(a, b, precision=PREC, preferred_element_type=jnp.float32)


def polynomial_of(gram):
    eye = jnp.eye(gram.shape[-1], dtype=jnp.float32)
    q = None
    s = gram
    for k in range(NS_ITERS):
        m = quintic_a * eye + quintic_b * s + quintic_c * mm(s, s)
        q = m if q is None else mm(q, m)
        if k < NS_ITERS - 1:
            s = mm(mm(s, m), m)
    return q


def shards(momentum, grad_one, grad_two):
    latent = momentum.shape[-1]
    one = (
        momentum_decay * momentum.astype(jnp.float32) + grad_one.astype(jnp.float32)
    ).astype(jnp.bfloat16)
    two = (
        momentum_decay * one.astype(jnp.float32) + grad_two.astype(jnp.float32)
    ).astype(jnp.bfloat16)
    team = lax.all_to_all(two, "layer", split_axis=0, concat_axis=1, tiled=True)[0]
    g2 = lax.psum(jnp.dot(team.T, team, preferred_element_type=jnp.float32), "head")
    n2 = jnp.sqrt(jnp.trace(g2)) + norm_epsilon
    q2 = polynomial_of(g2 / (n2 * n2)) * (math.sqrt(ROWS) / n2)
    q2 = lax.all_gather(q2, "layer", axis=0)
    g1 = jnp.einsum("nrl,nsl->nrs", one, one, preferred_element_type=jnp.float32)
    n1 = jnp.sqrt(jnp.trace(g1, axis1=1, axis2=2))[:, None, None] + norm_epsilon
    q1 = polynomial_of(g1 / (n1 * n1)) * (math.sqrt(max(HEAD_ROWS, latent)) / n1)
    update_one = mm(q1, one.astype(jnp.float32))
    update_two = mm(two.astype(jnp.float32), q2)
    return (update_one, update_two)


def solution(mesh):
    spec = P(None, ("layer", "head"), None)
    return jax.shard_map(
        shards, mesh=mesh, in_specs=(spec,) * 3, out_specs=(spec,) * 2, check_vma=False
    )
```

time: 346 us -> 223 us (0.64); the launches traced: 340 us -> 223 us
  blocking collectives: 151 us -> 18.9 us
  waiting for transfers between devices: 47.2 us -> 139 us
  matrix products: 79.5 us -> 45.3 us
  starting transfers between devices: 29.2 us -> 0.08 us
  local copies, waits for them, and re-layouts: 17.2 us -> 0.02 us
  between operations: 2.19 us -> 15.1 us
  other arithmetic: 13.1 us -> 4.33 us
    all_to_all x16 -> x1, blocking collectives: 151 us -> 18.9 us  [shards(): lax.all_to_all(two, 'layer', split_axis=0, concat_axis=1, tiled=True)[0]]
    psum x0 -> x1, waiting for transfers between devices: none -> 107 us  [shards(): lax.psum(jnp.dot(team.T, team, preferred_element_type=jnp.float32), 'head')]
    all_to_all x7 -> x0, waiting for transfers between devices: 47.2 us -> none  [the longest x3 19.7 us: sum_in_two_steps(): return jnp.sum(lax.all_to_all(own, far, 0, 0, tiled=True), axis=0)]
    dot_general x30 -> x38, matrix products: 79.5 us -> 45.3 us  [the longest x36 42.7 us: mm(): return jnp.matmul(a, b, precision=PREC, preferred_element_type=jnp.float32)]
    all_gather x0 -> x1, waiting for transfers between devices: none -> 31.7 us  [shards(): q2 = lax.all_gather(q2, 'layer', axis=0)]
    all_to_all x7 -> x0, starting transfers between devices: 29.2 us -> none  [the longest x3 12.9 us: copy_for_each(): return lax.all_to_all(copies, axis, split_axis=0, concat_axis=0, tiled=True)]
    broadcast_in_dim x12 -> x0, local copies, waits for them, and re-layouts: 9.53 us -> none  [the longest x11 6.03 us: copy_for_each(): copies = jnp.broadcast_to(x, (lax.axis_size(axis), *x.shape))]
    reduce_sum x13 -> x1, other arithmetic: 9.4 us -> 1.9 us  [shards(): n2 = jnp.sqrt(jnp.trace(g2)) + norm_epsilon]
  transfers between devices with their start and end apart: 7 -> 2, of which waited for: 7 -> 2; matrix products, arithmetic and copies ran while one was open for 10% -> 7% of each run, Pallas kernels for 0% -> 0%
where the time goes in v1:
time: 223 us
  waiting for transfers between devices  139 us (62%)
  matrix products  45.3 us (20%)
  blocking collectives  18.9 us (8%)
  between operations  15.1 us (7%)
  other arithmetic  4.33 us (2%)
    psum x1, waiting for transfers between devices, shards(): lax.psum(jnp.dot(team.T, team, preferred_element_type=jnp.float32), 'head')  107 us
    dot_general x36, matrix products, mm(): return jnp.matmul(a, b, precision=PREC, preferred_element_type=jnp.float32)  42.7 us
    all_gather x1, waiting for transfers between devices, shards(): q2 = lax.all_gather(q2, 'layer', axis=0)  31.7 us
    all_to_all x1, blocking collectives, shards(): lax.all_to_all(two, 'layer', split_axis=0, concat_axis=1, tiled=True)[0]  18.9 us
  transfers between devices with their start and end apart: 2, of which 2 were waited for; matrix products, arithmetic and copies ran while one was open for 7% of the time, Pallas kernels for 0%

profile of v1, /device:TPU:1, one launch (start us, length us, event | category | flops | bytes accessed | tf_op | source)
XLA Modules:
  0.0 222.8 jit_solution(18386275841103472611)
XLA Ops:
  7.2 2.4 %add_convert_fusion = bf16[4,256,512]{2,1,0:T(8,128)(2,1)S(1)} fusion(bf16[4,256,512]{2,1,0:T(8,128)(2,1)} %param.5, bf16[4,256,512]{2,1,0:T(8,128)(2,1)} %param.4, bf16[4,256,512]{2,1,0:T(8,128)(2,1)} %param.3), kind=kLoop, calls=%fused_computation.5 | loop fusion | flops 5242880 | bytes 4194304 | tf_op jit(solution)/shard_map/convert_element_type | solution.py:43
  9.6 18.9 %all_to_all.4 = bf16[4,256,512]{2,1,0:T(8,128)(2,1)S(1)} all-to-all(bf16[4,256,512]{2,1,0:T(8,128)(2,1)S(1)} %add_convert_fusion), channel_id=1, replica_groups=mesh['layer'=4,'head'=32] {'layer'}, dimensions={0} | all-to-all | bytes 2097152 | tf_op jit(solution)/shard_map/all_to_all | solution.py:44
  28.5 1.7 convolution_bitcast_fusion
  30.2 107.4 %all-reduce.2.cloned.1.call-done = f32[512,512]{1,0:T(8,128)} async-done(((f32[512,512]{1,0:T(8,128)}), f32[512,512]{1,0:T(8,128)}) %all-reduce.2.cloned.1.call-update) | async-done | bytes 1048592 | tf_op jit(solution)/shard_map/psum | solution.py:45
  137.7 1.9 select_reduce_fusion
  140.3 3.2 %fusion.4 = f32[512,512]{1,0:T(8,128)S(1)} fusion(f32[512,512]{1,0:T(8,128)} %all-reduce.2.cloned.1.call-done, f32[]{:T(128)S(6)} %mul.138), kind=kOutput, calls=%fused_computation.17 | convolution fusion | flops 807403520 | bytes 2097156 | tf_op jit(solution)/shard_map/dot_general | solution.py:21
  143.5 1.0 fusion.10
  144.5 1.0 fusion.25
  145.5 1.1 fusion.3
  146.6 2.0 fusion.27
  148.6 1.0 fusion.26
  149.6 2.2 %fusion.28 = f32[512,512]{1,0:T(8,128)S(1)} fusion(f32[512,512]{1,0:T(8,128)} %fusion.27, f32[512,512]{1,0:T(8,128)S(1)} %fusion.3), kind=kOutput, calls=%fused_computation.57 | convolution fusion | flops 805306368 | bytes 3145728 | tf_op jit(solution)/shard_map/dot_general | solution.py:21
  151.9 1.1 fusion.2
  152.9 1.0 fusion.30
  154.0 1.0 fusion.31
  155.0 1.0 fusion.29
  156.0 1.1 fusion.1
  157.0 1.2 fusion.33
  158.3 1.0 fusion.34
  159.3 1.0 fusion.32
  160.3 1.1 fusion
  161.4 2.0 convolution_multiply_fusion
  163.5 0.9 select_reduce_fusion.1
  164.4 0.9 fusion.9
  166.7 0.8 fusion.8
  169.6 0.8 fusion.7
  171.9 0.9 fusion.19
  172.8 0.8 fusion.6
  175.7 0.8 fusion.5
  177.3 2.1 fusion.13
  179.4 31.7 %all-gather.3.cloned.1.call-done = f32[2048,512]{1,0:T(8,128)} async-done(((f32[512,512]{1,0:T(8,128)}), f32[2048,512]{1,0:T(8,128)}) %all-gather.3.cloned.1.call-update) | async-done | bytes 4194320 | tf_op jit(solution)/shard_map/all_gather | solution.py:48
  211.1 4.9 %fusion.35 = f32[4,256,512]{2,1,0:T(8,128)} fusion(bf16[4,256,512]{2,1,0:T(8,128)(2,1)S(1)} %add_convert_fusion, f32[4,512,512]{2,1,0:T(8,128)} %bitcast.70), kind=kOutput, calls=%fused_computation.64 | convolution fusion | flops 1610612736 | bytes 7340032 | tf_op jit(solution)/shard_map/dot_general | solution.py:21
  (24 shorter events, 7.8 us)
Async XLA Ops:
  7.2 130.5 %all-reduce.2.cloned.1.call-start = ((), (), s32[]{:S(2)}) async-start(), calls=%async_computation.1 | async-start | bytes 2097152 | tf_op jit(solution)/shard_map/psum | solution.py:45
  30.2 180.9 %all-gather.3.cloned.1.call-start = ((), (), s32[]{:S(2)}) async-start(), calls=%async_computation.2 | async-start | bytes 5242880 | tf_op jit(solution)/shard_map/all_gather | solution.py:48
  140.2 3.2 %copy-start.2 = (f32[512,512]{1,0:T(8,128)S(1)}, f32[512,512]{1,0:T(8,128)}, u32[]{:S(2)}) copy-start(f32[512,512]{1,0:T(8,128)} %all-reduce.2.cloned.1.call-done) | copy-start | bytes 3145732
  161.4 2.1 copy-start
  161.4 2.1 copy-start.1
Sparse Core Ops, SparseCore 0:
  30.3 107.2 all-reduce.1
  163.5 47.5 all-gather.2

commit v2 on v1

v2 whole, which is shorter than its diff:
```python
import functools
import math

import jax
import jax.numpy as jnp
from jax import lax
from jax.experimental import pallas as pl
from jax.experimental.pallas import tpu as pltpu
from jax.sharding import PartitionSpec as P

NS_ITERS = 5
quintic_a = 3.4445
quintic_b = -4.775
quintic_c = 2.0315
norm_epsilon = 1e-07
momentum_decay = 0.95

bf16 = jnp.bfloat16
f32 = jnp.float32
MESH = pl.DeviceIdType.MESH
LAYERS, ROWS, LATENT = 4, 256, 512
ALL_ROWS = 32768
T = 128
BLOCKS = [(i, j) for i in range(4) for j in range(i, 4)]
HALF = len(BLOCKS) * T // 2
PIECE = HALF // 16
OFFSETS = [(1, 1, 2), (1, 1, 0), (1, 0, 2), (0, 1, 2)]
OFFSETS += [(i, j, z) for z in (1, 3) for i in (0, 1) for j in (0, 1)]
OFFSETS += [(1, 0, 0), (0, 1, 0), (0, 0, 2)]


def split(x):
    high = x.astype(bf16)
    return high, (x - high.astype(f32)).astype(bf16)


def dot(x, y):
    return jnp.dot(x, y, preferred_element_type=f32)


def dot3(x, y):
    return dot(x[0], y[0]) + (dot(x[0], y[1]) + dot(x[1], y[0]))


def mm(x, y):
    return dot3(x, y)


def mm_even(x, y):
    h = x[0].shape[0] // 2
    top = dot3([t[:h] for t in x], y)
    low = dot3([t[h:] for t in x], [t[:, h:] for t in y])
    return jnp.concatenate([top, jnp.concatenate([top[:, h:].T, low], 1)], 0)


def eye(n):
    rows = lax.broadcasted_iota(jnp.int32, (n, n), 0)
    return rows == lax.broadcasted_iota(jnp.int32, (n, n), 1)


def polynomials(grams, product):
    n = grams[0].shape[0]
    diag = jnp.where(eye(n), f32(quintic_a), f32(0.0))
    s, q = list(grams), [None] * len(grams)
    for k in range(NS_ITERS):
        parts = [split(t) for t in s]
        m = [
            diag + (quintic_b * t + quintic_c * product(u, u)) for t, u in zip(s, parts)
        ]
        ms = [split(t) for t in m]
        if k < NS_ITERS - 1:
            r = [split(product(u, v)) for u, v in zip(parts, ms)]
            s = [product(u, v) for u, v in zip(r, ms)]
        q = m if k == 0 else [product(split(u), v) for u, v in zip(q, ms)]
    return q


def trace(x):
    return jnp.sum(jnp.where(eye(x.shape[0]), x, f32(0.0)))


def exchange(
    m_ref, g1_ref, g2_ref, y1_ref, y2_ref, q1_ref, q2_ref,
    rx, part, core_in, own, rs, gath, packed, rxq,
    s_row, r_row, s_core, r_core, s_rs, r_rs, s_ag, r_ag, s_rel, r_rel, s_q, r_q,
):
    x = lax.axis_index("layer")
    head = lax.axis_index("head")
    y, z, c = head // 8, (head // 2) % 4, head % 2
    b0, b1 = (x + z) % 2, (y + z) % 2
    lay = b0 + 2 * b1
    lays = [(1 - b0) + 2 * b1, b0 + 2 * (1 - b1), (1 - b0) + 2 * (1 - b1)]
    i, j = x // 2, y // 2
    t = (i * 2 + j) * 4 + z

    def at(x, y, z, c):
        return (x, (y * 4 + z) * 2 + c)

    steps = []
    for a in range(3):
        for s in range(2):
            d = 1 if s == 0 else 3
            steps.append(((x + d) % 4 if a == 0 else x, (y + d) % 4 if a == 1 else y,
                          (z + d) % 4 if a == 2 else z))
    team = []
    for di, dj, dz in OFFSETS:
        i2, j2, z2 = (i + di) % 2, (j + dj) % 2, (z + dz) % 4
        team.append(((2 * i2 + (b0 + z2) % 2, 2 * j2 + (b1 + z2) % 2, z2),
                     (i2 * 2 + j2) * 4 + z2))
    partner = at(x, y, z, 1 - c)

    barrier = pltpu.get_barrier_semaphore()
    greet = [partner]
    greet += [at(*p, k) for p in steps for k in (c, 1 - c)]
    greet += [at(*p, c) for p, _ in team]
    for who in greet:
        pl.semaphore_signal(barrier, inc=1, device_id=who, device_id_type=MESH)

    for n in range(LAYERS):
        one = (momentum_decay * m_ref[n].astype(f32) + g1_ref[n].astype(f32)).astype(bf16)
        y1_ref[n] = one
        y2_ref[n] = (momentum_decay * one.astype(f32) + g2_ref[n].astype(f32)).astype(bf16)

    pl.semaphore_wait(barrier, len(greet))

    def send(src, dst, ss, rr, who):
        return pltpu.make_async_remote_copy(
            src_ref=src, dst_ref=dst, send_sem=ss, recv_sem=rr, device_id=who,
            device_id_type=MESH)

    row_copies = []
    for k, p in enumerate(steps):
        row_copies.append(send(
            y2_ref.at[lays[k // 2], pl.ds((k % 2) * 128, 128), :], rx.at[k],
            s_row.at[k], r_row.at[k], at(*p, c)))
    for copy in row_copies:
        copy.start()

    def heads(ns):
        grams = []
        norms = []
        for n in ns:
            v = y1_ref[n]
            g = lax.dot_general(v, v, (((1,), (1,)), ((), ())), preferred_element_type=f32)
            norm = jnp.sqrt(trace(g)) + norm_epsilon
            grams.append(g * (1.0 / (norm * norm)))
            norms.append(norm)
        for n, q, norm in zip(ns, polynomials(grams, mm), norms):
            high, low = split(q * (math.sqrt(max(ROWS, LATENT)) / norm))
            q1_ref[n, 0] = high
            q1_ref[n, 1] = low

    heads((0, 1))
    for copy in row_copies:
        copy.wait()

    def gram_rows(i):
        total = None
        for v in [y2_ref.at[lay]] + [rx.at[k] for k in range(6)]:
            left = v[:, pl.ds(i * T, T)]
            right = v[:, pl.ds(i * T, LATENT - i * T)]
            g = lax.dot_general(left, right, (((0,), (0,)), ((), ())), preferred_element_type=f32)
            total = g if total is None else total + g
        return total

    for i4 in range(4):
        g = gram_rows(i4)
        for j4 in range(i4, 4):
            b = BLOCKS.index((i4, j4))
            part[pl.ds(b * T, T), :] = g[:, (j4 - i4) * T:(j4 - i4 + 1) * T]

    theirs = pl.ds(pl.multiple_of((1 - c) * HALF, 8), HALF)
    mine = pl.ds(pl.multiple_of(c * HALF, 8), HALF)
    swap = send(part.at[theirs, :], core_in, s_core, r_core, partner)
    swap.start()
    swap.wait()
    own[...] = part[mine, :] + core_in[...]

    rs_copies = []
    for k, (p, t2) in enumerate(team):
        rs_copies.append(send(
            own.at[pl.ds(pl.multiple_of(t2 * PIECE, 8), PIECE), :], rs.at[k],
            s_rs.at[k], r_rs.at[k], at(*p, c)))
    for copy in rs_copies:
        copy.start()
    heads((2, 3))
    for copy in rs_copies:
        copy.wait()
    total = own[pl.ds(pl.multiple_of(t * PIECE, 8), PIECE), :]
    for k in range(15):
        total = total + rs[k]
    here = pl.ds(pl.multiple_of(c * HALF + t * PIECE, 8), PIECE)
    gath[here, :] = total
    ag_copies = [
        send(gath.at[here, :], gath.at[here, :], s_ag.at[k], r_ag.at[k], at(*p, c))
        for k, (p, _) in enumerate(team)
    ]
    for copy in ag_copies:
        copy.start()
    for copy in ag_copies:
        copy.wait_send()
    for k in range(15):
        di, dj, dz = OFFSETS[k]
        t3 = (((i + di) % 2) * 2 + (j + dj) % 2) * 4 + (z + 4 - dz) % 4
        there = pl.ds(pl.multiple_of(c * HALF + t3 * PIECE, 8), PIECE)
        send(gath.at[there, :], gath.at[there, :], s_ag.at[k], r_ag.at[k],
             at(*team[k][0], c)).wait_recv()
    relay = send(gath.at[mine, :], gath.at[mine, :], s_rel, r_rel, partner)
    relay.start()
    relay.wait_send()
    send(gath.at[theirs, :], gath.at[theirs, :], s_rel, r_rel, partner).wait_recv()

    tiles = {}
    for b, (bi, bj) in enumerate(BLOCKS):
        v = gath[pl.ds(b * T, T), :]
        tiles[bi, bj] = v
        if bi != bj:
            tiles[bj, bi] = v.T
    gram = jnp.concatenate(
        [jnp.concatenate([tiles[r, k] for k in range(4)], 1) for r in range(4)], 0)
    norm = jnp.sqrt(trace(gram)) + norm_epsilon
    q = polynomials([gram * (1.0 / (norm * norm))], mm_even)[0]
    parts = split(q * (math.sqrt(ALL_ROWS) / norm))
    for k in range(2):
        q2_ref[lay, k] = parts[k]
        packed[k, 0:256, :] = parts[k][0:256, :]
        packed[k, 256:384, 0:256] = parts[k][256:384, 256:512]
        packed[k, 256:384, 256:512] = parts[k][384:512, 256:512]
    q_copies = []
    for k, p in enumerate(steps):
        rows = pl.ds(pl.multiple_of((k % 2) * 192 + c * 96, 16), 96)
        for d in range(2):
            q_copies.append(send(
                packed.at[:, rows, :], rxq.at[k // 2, :, rows, :], s_q.at[k, d],
                r_q.at[k, c], at(*p, d)))
    for copy in q_copies:
        copy.start()
    for copy in q_copies:
        copy.wait_send()
    for k, p in enumerate(steps):
        for d in range(2):
            rows = pl.ds((k % 2) * 192 + d * 96, 96)
            send(packed.at[:, rows, :], rxq.at[k // 2, :, rows, :], s_q.at[k, d],
                 r_q.at[k, d], at(*p, d)).wait_recv()
    for a in range(3):
        for k in range(2):
            top = rxq[a, k, 0:256, :]
            q2_ref[lays[a], k, 0:256, :] = top
            q2_ref[lays[a], k, 256:512, 0:256] = top[:, 256:512].T
            q2_ref[lays[a], k, 256:384, 256:512] = rxq[a, k, 256:384, 0:256]
            q2_ref[lays[a], k, 384:512, 256:512] = rxq[a, k, 256:384, 256:512]


def finish(y1_ref, y2_ref, q1_ref, q2_ref, o1_ref, o2_ref):
    v = y1_ref[0]
    o1_ref[0] = dot(q1_ref[0, 0], v) + dot(q1_ref[0, 1], v)
    w = y2_ref[0]
    o2_ref[0] = dot(w, q2_ref[0, 0]) + dot(w, q2_ref[0, 1])


def shards(momentum, grad_one, grad_two):
    vmem = pl.BlockSpec(memory_space=pltpu.VMEM)
    dma = pltpu.SemaphoreType.DMA
    y1, y2, q1, q2 = pl.pallas_call(
        exchange,
        out_shape=(
            jax.ShapeDtypeStruct((LAYERS, ROWS, LATENT), bf16),
            jax.ShapeDtypeStruct((LAYERS, ROWS, LATENT), bf16),
            jax.ShapeDtypeStruct((LAYERS, 2, ROWS, ROWS), bf16),
            jax.ShapeDtypeStruct((LAYERS, 2, LATENT, LATENT), bf16),
        ),
        in_specs=[vmem] * 3,
        out_specs=(vmem,) * 4,
        scratch_shapes=[
            pltpu.VMEM((6, 128, LATENT), bf16),
            pltpu.VMEM((2 * HALF, T), f32),
            pltpu.VMEM((HALF, T), f32),
            pltpu.VMEM((HALF, T), f32),
            pltpu.VMEM((15, PIECE, T), f32),
            pltpu.VMEM((2 * HALF, T), f32),
            pltpu.VMEM((2, 384, LATENT), bf16),
            pltpu.VMEM((3, 2, 384, LATENT), bf16),
            dma((6,)), dma((6,)), dma, dma, dma((15,)), dma((15,)), dma((15,)), dma((15,)),
            dma, dma, dma((6, 2)), dma((6, 2)),
        ],
        compiler_params=pltpu.CompilerParams(
            collective_id=0, has_side_effects=True, vmem_limit_bytes=56 << 20),
        name="exchange",
    )(momentum, grad_one, grad_two)

    def block(*shape):
        return pl.BlockSpec((1, *shape), lambda n: (n,) + (0,) * len(shape))

    return pl.pallas_call(
        finish,
        grid=(LAYERS,),
        out_shape=(jax.ShapeDtypeStruct((LAYERS, ROWS, LATENT), f32),) * 2,
        in_specs=[block(ROWS, LATENT), block(ROWS, LATENT), block(2, ROWS, ROWS),
                  block(2, LATENT, LATENT)],
        out_specs=(block(ROWS, LATENT),) * 2,
        name="finish",
    )(y1, y2, q1, q2)


def solution(mesh):
    spec = P(None, ("layer", "head"), None)
    return jax.shard_map(
        shards, mesh=mesh, in_specs=(spec,) * 3, out_specs=(spec,) * 2, check_vma=False
    )
```

time: 223 us -> 70.5 us (0.32)
  waiting for transfers between devices: 139 us -> 0 us
  Pallas kernels: 0 us -> 69.6 us
  matrix products: 45.3 us -> 0 us
  blocking collectives: 18.9 us -> 0 us
  between operations: 15.1 us -> 0.64 us
  other arithmetic: 4.33 us -> 0 us
    psum x1 -> x0, waiting for transfers between devices: 107 us -> none  [shards(): lax.psum(jnp.dot(team.T, team, preferred_element_type=jnp.float32), 'head')]
    pallas_call x0 -> x2, Pallas kernels: none -> 69.6 us  [the longest x1 63.6 us: shards(): pl.pallas_call(exchange, out_shape=(jax.ShapeDtypeStruct((LAYERS, ROWS, L...]
    dot_general x38 -> x0, matrix products: 45.3 us -> none  [the longest x36 42.7 us: mm(): return jnp.matmul(a, b, precision=PREC, preferred_element_type=jnp.float32)]
    all_gather x1 -> x0, waiting for transfers between devices: 31.7 us -> none  [shards(): q2 = lax.all_gather(q2, 'layer', axis=0)]
    all_to_all x1 -> x0, blocking collectives: 18.9 us -> none  [shards(): lax.all_to_all(two, 'layer', split_axis=0, concat_axis=1, tiled=True)[0]]
    convert_element_type x1 -> x0, other arithmetic: 2.37 us -> none  [shards(): two = (momentum_decay * one.astype(jnp.float32) + grad_two.astype(jnp.flo...]
  transfers between devices with their start and end apart: 2 -> 0, of which waited for: 2 -> 0; matrix products, arithmetic and copies ran while one was open for 7% -> 0% of each run, Pallas kernels for 0% -> 0%
where the time goes in v2:
time: 70.5 us; the launch traced here: 70.3 us
  Pallas kernels  69.6 us (99%)
    pallas_call x1, Pallas kernels, shards(): pl.pallas_call(exchange, out_shape=(jax.ShapeDtypeStruct((LAYERS, ROWS, L...  63.6 us
    pallas_call x1, Pallas kernels, shards(): pl.pallas_call(finish, grid=(LAYERS,), out_shape=(jax.ShapeDtypeStruct((L...  6.08 us

profile of v2, /device:TPU:1, one launch (start us, length us, event | category | flops | bytes accessed | tf_op | source)
XLA Modules:
  0.0 70.3 jit_solution(522869799974027513)
XLA Ops:
  0.6 63.6 %exchange.1 = (bf16[4,256,512]{2,1,0:T(8,128)(2,1)}, bf16[4,256,512]{2,1,0:T(8,128)(2,1)}, bf16[4,2,256,256]{3,2,1,0:T(8,128)(2,1)}, bf16[4,2,512,512]{3,2,1,0:T(8,128)(2,1)}) custom-call(bf16[4,256,512]{2,1,0:T(8,128)(2,1)} %m_ref.1, bf16[4,256,512]{2,1,0:T(8,128)(2,1)} %g1_ref.1, bf16[4,256,512]{2,1,0:T(8,128)(2,1)} %g2_ref.1), custom_call_target="tpu_custom_call" | custom-call | tf_op jit(solution)/shard_map/exchange/pallas_call | solution.py:264
  64.2 6.1 %finish.1 = (f32[4,256,512]{2,1,0:T(8,128)}, f32[4,256,512]{2,1,0:T(8,128)}) custom-call(bf16[4,256,512]{2,1,0:T(8,128)(2,1)} %get-tuple-element.6.y1_ref, bf16[4,256,512]{2,1,0:T(8,128)(2,1)} %get-tuple-element.7.y2_ref, bf16[4,2,256,256]{3,2,1,0:T(8,128)(2,1)} %get-tuple-element.8.q1_ref, bf16[4,2,512,512]{3,2,1,0:T(8,128)(2,1)} %get-tuple-element.9.q2_ref), custom_call_target="tpu_custom_call" | custom-call | tf_op jit(solution)/shard_map/finish/pallas_call | solution.py:294

commit v3 on v2

--- a/solution.py
+++ b/solution.py
@@ -24,6 +24,9 @@
 BLOCKS = [(i, j) for i in range(4) for j in range(i, 4)]
 HALF = len(BLOCKS) * T // 2
 PIECE = HALF // 16
+QUARTER = HALF // 2
+SHARES = 2
+SHARE = QUARTER // SHARES
 OFFSETS = [(1, 1, 2), (1, 1, 0), (1, 0, 2), (0, 1, 2)]
 OFFSETS += [(i, j, z) for z in (1, 3) for i in (0, 1) for j in (0, 1)]
 OFFSETS += [(1, 0, 0), (0, 1, 0), (0, 0, 2)]
@@ -75,14 +78,26 @@
     return q
 
 
+def unpacked(blocks):
+    tiles = {}
+    for b, (i, j) in enumerate(BLOCKS):
+        v = blocks[b * T:(b + 1) * T, :]
+        tiles[i, j] = v
+        if i != j:
+            tiles[j, i] = v.T
+    return jnp.concatenate(
+        [jnp.concatenate([tiles[i, j] for j in range(4)], 1) for i in range(4)], 0)
+
+
 def trace(x):
     return jnp.sum(jnp.where(eye(x.shape[0]), x, f32(0.0)))
 
 
 def exchange(
-    m_ref, g1_ref, g2_ref, y1_ref, y2_ref, q1_ref, q2_ref,
-    rx, part, core_in, own, rs, gath, packed, rxq,
-    s_row, r_row, s_core, r_core, s_rs, r_rs, s_ag, r_ag, s_rel, r_rel, s_q, r_q,
+    m_hbm, g1_hbm, g2_hbm, o1_ref, o2_ref,
+    ins, y1_ref, y2_ref, q1_ref, rx, part, core_in, own, rs, gath, packed, rxq,
+    s_in, s_row, r_row, s_core, r_core, s_rs, r_rs, s_ag, r_ag, s_rel, r_rel,
+    s_q, r_q, s_qr, r_qr,
 ):
     x = lax.axis_index("layer")
     head = lax.axis_index("head")
@@ -109,17 +124,27 @@
                      (i2 * 2 + j2) * 4 + z2))
     partner = at(x, y, z, 1 - c)
 
+    loads = [
+        [pltpu.make_async_copy(h.at[n], ins.at[k, n], s_in.at[k, n])
+         for k, h in enumerate((m_hbm, g1_hbm, g2_hbm))]
+        for n in range(LAYERS)
+    ]
+    for group in loads:
+        for copy in group:
+            copy.start()
     barrier = pltpu.get_barrier_semaphore()
     greet = [partner]
-    greet += [at(*p, k) for p in steps for k in (c, 1 - c)]
+    greet += [at(*p, c) for p in steps]
     greet += [at(*p, c) for p, _ in team]
     for who in greet:
         pl.semaphore_signal(barrier, inc=1, device_id=who, device_id_type=MESH)
 
     for n in range(LAYERS):
-        one = (momentum_decay * m_ref[n].astype(f32) + g1_ref[n].astype(f32)).astype(bf16)
+        for copy in loads[n]:
+            copy.wait()
+        one = (momentum_decay * ins[0, n].astype(f32) + ins[1, n].astype(f32)).astype(bf16)
         y1_ref[n] = one
-        y2_ref[n] = (momentum_decay * one.astype(f32) + g2_ref[n].astype(f32)).astype(bf16)
+        y2_ref[n] = (momentum_decay * one.astype(f32) + ins[2, n].astype(f32)).astype(bf16)
 
     pl.semaphore_wait(barrier, len(greet))
 
@@ -150,7 +175,6 @@
             q1_ref[n, 0] = high
             q1_ref[n, 1] = low
 
-    heads((0, 1))
     for copy in row_copies:
         copy.wait()
 
@@ -183,7 +207,7 @@
             s_rs.at[k], r_rs.at[k], at(*p, c)))
     for copy in rs_copies:
         copy.start()
-    heads((2, 3))
+    heads((0, 1))
     for copy in rs_copies:
         copy.wait()
     total = own[pl.ds(pl.multiple_of(t * PIECE, 8), PIECE), :]
@@ -197,109 +221,101 @@
     ]
     for copy in ag_copies:
         copy.start()
+    heads((2, 3))
+
+    def relay(k, t3, core):
+        there = pl.ds(pl.multiple_of(core * HALF + t3 * PIECE, 8), PIECE)
+        return send(gath.at[there, :], gath.at[there, :], s_rel.at[k], r_rel.at[k], partner)
+
+    relays = [(15, t)]
+    for k, (di, dj, dz) in enumerate(OFFSETS):
+        relays.append((k, (((i + di) % 2) * 2 + (j + dj) % 2) * 4 + (z + 4 - dz) % 4))
+    for k, t3 in [relays[0]] + relays[:0:-1]:
+        if k < 15:
+            there = pl.ds(pl.multiple_of(c * HALF + t3 * PIECE, 8), PIECE)
+            send(gath.at[there, :], gath.at[there, :], s_ag.at[k], r_ag.at[k],
+                 at(*team[k][0], c)).wait_recv()
+        relay(k, t3, c).start()
     for copy in ag_copies:
         copy.wait_send()
-    for k in range(15):
-        di, dj, dz = OFFSETS[k]
-        t3 = (((i + di) % 2) * 2 + (j + dj) % 2) * 4 + (z + 4 - dz) % 4
-        there = pl.ds(pl.multiple_of(c * HALF + t3 * PIECE, 8), PIECE)
-        send(gath.at[there, :], gath.at[there, :], s_ag.at[k], r_ag.at[k],
-             at(*team[k][0], c)).wait_recv()
-    relay = send(gath.at[mine, :], gath.at[mine, :], s_rel, r_rel, partner)
-    relay.start()
-    relay.wait_send()
-    send(gath.at[theirs, :], gath.at[theirs, :], s_rel, r_rel, partner).wait_recv()
-
-    tiles = {}
-    for b, (bi, bj) in enumerate(BLOCKS):
-        v = gath[pl.ds(b * T, T), :]
-        tiles[bi, bj] = v
-        if bi != bj:
-            tiles[bj, bi] = v.T
-    gram = jnp.concatenate(
-        [jnp.concatenate([tiles[r, k] for k in range(4)], 1) for r in range(4)], 0)
+    for k, t3 in relays:
+        relay(k, t3, c).wait_send()
+    for k, t3 in relays:
+        relay(k, t3, 1 - c).wait_recv()
+
+    gram = unpacked(gath[...])
     norm = jnp.sqrt(trace(gram)) + norm_epsilon
     q = polynomials([gram * (1.0 / (norm * norm))], mm_even)[0]
     parts = split(q * (math.sqrt(ALL_ROWS) / norm))
     for k in range(2):
-        q2_ref[lay, k] = parts[k]
-        packed[k, 0:256, :] = parts[k][0:256, :]
-        packed[k, 256:384, 0:256] = parts[k][256:384, 256:512]
-        packed[k, 256:384, 256:512] = parts[k][384:512, 256:512]
-    q_copies = []
-    for k, p in enumerate(steps):
-        rows = pl.ds(pl.multiple_of((k % 2) * 192 + c * 96, 16), 96)
-        for d in range(2):
-            q_copies.append(send(
-                packed.at[:, rows, :], rxq.at[k // 2, :, rows, :], s_q.at[k, d],
-                r_q.at[k, c], at(*p, d)))
+        for b, (bi, bj) in enumerate(BLOCKS):
+            packed[k, b * T:(b + 1) * T, :] = parts[k][bi * T:(bi + 1) * T, bj * T:(bj + 1) * T]
+
+    def part_of(a, s, h, core, src, ss, rr, who):
+        rows = pl.ds(pl.multiple_of((s * 2 + core) * QUARTER + h * SHARE, 16), SHARE)
+        return send(src.at[:, rows, :], rxq.at[a, :, rows, :], ss.at[a, s, h], rr.at[a, s, h], who)
+
+    order = [(a, s, h) for h in range(SHARES) for a in range(3) for s in range(2)]
+    q_copies = [
+        part_of(a, s, h, c, packed, s_q, r_q, at(*steps[2 * a + s], c)) for a, s, h in order
+    ]
     for copy in q_copies:
         copy.start()
-    for copy in q_copies:
+    w = y2_ref[lay]
+    o2_ref[lay] = dot(w, parts[0]) + dot(w, parts[1])
+    for n in range(LAYERS):
+        v = y1_ref[n]
+        o1_ref[n] = dot(q1_ref[n, 0], v) + dot(q1_ref[n, 1], v)
+    passed = []
+    for copy, (a, s, h) in zip(q_copies, order):
+        copy.wait()
+        passed.append(part_of(a, s, h, c, rxq.at[a], s_qr, r_qr, partner))
+        passed[-1].start()
+    for copy in passed:
         copy.wait_send()
-    for k, p in enumerate(steps):
-        for d in range(2):
-            rows = pl.ds((k % 2) * 192 + d * 96, 96)
-            send(packed.at[:, rows, :], rxq.at[k // 2, :, rows, :], s_q.at[k, d],
-                 r_q.at[k, d], at(*p, d)).wait_recv()
     for a in range(3):
+        for s in range(2):
+            for h in range(SHARES):
+                part_of(a, s, h, 1 - c, rxq.at[a], s_qr, r_qr, partner).wait_recv()
+        w = y2_ref[lays[a]]
+        total = None
         for k in range(2):
-            top = rxq[a, k, 0:256, :]
-            q2_ref[lays[a], k, 0:256, :] = top
-            q2_ref[lays[a], k, 256:512, 0:256] = top[:, 256:512].T
-            q2_ref[lays[a], k, 256:384, 256:512] = rxq[a, k, 256:384, 0:256]
-            q2_ref[lays[a], k, 384:512, 256:512] = rxq[a, k, 256:384, 256:512]
-
-
-def finish(y1_ref, y2_ref, q1_ref, q2_ref, o1_ref, o2_ref):
-    v = y1_ref[0]
-    o1_ref[0] = dot(q1_ref[0, 0], v) + dot(q1_ref[0, 1], v)
-    w = y2_ref[0]
-    o2_ref[0] = dot(w, q2_ref[0, 0]) + dot(w, q2_ref[0, 1])
+            full = unpacked(rxq[a, k])
+            term = dot(w, full)
+            total = term if total is None else total + term
+        o2_ref[lays[a]] = total
 
 
 def shards(momentum, grad_one, grad_two):
     vmem = pl.BlockSpec(memory_space=pltpu.VMEM)
+    hbm = pl.BlockSpec(memory_space=pltpu.MemorySpace.HBM)
     dma = pltpu.SemaphoreType.DMA
-    y1, y2, q1, q2 = pl.pallas_call(
+    return pl.pallas_call(
         exchange,
-        out_shape=(
-            jax.ShapeDtypeStruct((LAYERS, ROWS, LATENT), bf16),
-            jax.ShapeDtypeStruct((LAYERS, ROWS, LATENT), bf16),
-            jax.ShapeDtypeStruct((LAYERS, 2, ROWS, ROWS), bf16),
-            jax.ShapeDtypeStruct((LAYERS, 2, LATENT, LATENT), bf16),
-        ),
-        in_specs=[vmem] * 3,
-        out_specs=(vmem,) * 4,
+        out_shape=(jax.ShapeDtypeStruct((LAYERS, ROWS, LATENT), f32),) * 2,
+        in_specs=[hbm] * 3,
+        out_specs=(vmem,) * 2,
         scratch_shapes=[
+            pltpu.VMEM((3, LAYERS, ROWS, LATENT), bf16),
+            pltpu.VMEM((LAYERS, ROWS, LATENT), bf16),
+            pltpu.VMEM((LAYERS, ROWS, LATENT), bf16),
+            pltpu.VMEM((LAYERS, 2, ROWS, ROWS), bf16),
             pltpu.VMEM((6, 128, LATENT), bf16),
             pltpu.VMEM((2 * HALF, T), f32),
             pltpu.VMEM((HALF, T), f32),
             pltpu.VMEM((HALF, T), f32),
             pltpu.VMEM((15, PIECE, T), f32),
             pltpu.VMEM((2 * HALF, T), f32),
-            pltpu.VMEM((2, 384, LATENT), bf16),
-            pltpu.VMEM((3, 2, 384, LATENT), bf16),
-            dma((6,)), dma((6,)), dma, dma, dma((15,)), dma((15,)), dma((15,)), dma((15,)),
-            dma, dma, dma((6, 2)), dma((6, 2)),
+            pltpu.VMEM((2, 2 * HALF, T), bf16),
+            pltpu.VMEM((3, 2, 2 * HALF, T), bf16),
+            dma((3, LAYERS)), dma((6,)), dma((6,)), dma, dma,
+            dma((15,)), dma((15,)), dma((15,)), dma((15,)), dma((16,)), dma((16,)),
+            dma((3, 2, SHARES)), dma((3, 2, SHARES)), dma((3, 2, SHARES)), dma((3, 2, SHARES)),
         ],
         compiler_params=pltpu.CompilerParams(
-            collective_id=0, has_side_effects=True, vmem_limit_bytes=56 << 20),
+            collective_id=0, has_side_effects=True, vmem_limit_bytes=59 << 20),
         name="exchange",
     )(momentum, grad_one, grad_two)
-
-    def block(*shape):
-        return pl.BlockSpec((1, *shape), lambda n: (n,) + (0,) * len(shape))
-
-    return pl.pallas_call(
-        finish,
-        grid=(LAYERS,),
-        out_shape=(jax.ShapeDtypeStruct((LAYERS, ROWS, LATENT), f32),) * 2,
-        in_specs=[block(ROWS, LATENT), block(ROWS, LATENT), block(2, ROWS, ROWS),
-                  block(2, LATENT, LATENT)],
-        out_specs=(block(ROWS, LATENT),) * 2,
-        name="finish",
-    )(y1, y2, q1, q2)
 
 
 def solution(mesh):

time: 70.5 us -> 74.2 us (1.052)
  local copies, waits for them, and re-layouts: 0 us -> 4.55 us
    pallas_call x1 -> x0, Pallas kernels: 6.08 us -> none  [shards(): pl.pallas_call(finish, grid=(LAYERS,), out_shape=(jax.ShapeDtypeStruct((L...]
    pallas_call x1, Pallas kernels: 63.6 us -> 68.9 us  [shards(): pl.pallas_call(exchange, out_shape=(jax.ShapeDtypeStruct((LAYERS, ROWS, L...]
    unnamed x0 -> x4, local copies, waits for them, and re-layouts: none -> 4.55 us
where the time goes in v3:
time: 74.2 us; the launch traced here: 74.1 us
  Pallas kernels  68.9 us (93%)
  local copies, waits for them, and re-layouts  4.55 us (6%)
    pallas_call x1, Pallas kernels, shards(): pl.pallas_call(exchange, out_shape=(jax.ShapeDtypeStruct((LAYERS, ROWS, L...  68.9 us
    unnamed x4, local copies, waits for them, and re-layouts  4.55 us

profile of v3, /device:TPU:1, one launch (start us, length us, event | category | flops | bytes accessed | tf_op | source)
XLA Modules:
  0.0 74.1 jit_solution(3538196680153429902)
XLA Ops:
  0.6 68.9 %exchange.1 = (f32[4,256,512]{2,1,0:T(8,128)}, f32[4,256,512]{2,1,0:T(8,128)}) custom-call(bf16[4,256,512]{2,1,0:T(8,128)(2,1)} %m_hbm.1, bf16[4,256,512]{2,1,0:T(8,128)(2,1)} %g1_hbm.1, bf16[4,256,512]{2,1,0:T(8,128)(2,1)} %g2_hbm.1), custom_call_target="tpu_custom_call" | custom-call | tf_op jit(solution)/shard_map/exchange/pallas_call | solution.py:293
  69.5 0.0 copy-start
  69.5 3.2 %copy.7 = f32[4,256,512]{2,1,0:T(8,128)} copy(f32[4,256,512]{2,1,0:T(8,128)} %get-tuple-element.4) | data formatting | bytes 4194304
  72.7 0.0 copy-done
  72.8 1.3 %copy.8 = f32[4,256,512]{2,1,0:T(8,128)} copy(f32[4,256,512]{2,1,0:T(8,128)S(1)} %copy-done) | data formatting | bytes 4194304
Async XLA Ops:
  69.5 3.2 %copy-start = (f32[4,256,512]{2,1,0:T(8,128)S(1)}, f32[4,256,512]{2,1,0:T(8,128)}, u32[]{:S(2)}) copy-start(f32[4,256,512]{2,1,0:T(8,128)} %get-tuple-element.5) | copy-start | bytes 6291460

commit v4 on v3

--- a/solution.py
+++ b/solution.py
@@ -94,8 +94,8 @@
 
 
 def exchange(
-    m_hbm, g1_hbm, g2_hbm, o1_ref, o2_ref,
-    ins, y1_ref, y2_ref, q1_ref, rx, part, core_in, own, rs, gath, packed, rxq,
+    m_hbm, g1_hbm, g2_hbm, o1_ref, own2_ref, y2_ref, rxq,
+    ins, y1_ref, q1_ref, rx, part, core_in, own, rs, gath, packed,
     s_in, s_row, r_row, s_core, r_core, s_rs, r_rs, s_ag, r_ag, s_rel, r_rel,
     s_q, r_q, s_qr, r_qr,
 ):
@@ -262,7 +262,7 @@
     for copy in q_copies:
         copy.start()
     w = y2_ref[lay]
-    o2_ref[lay] = dot(w, parts[0]) + dot(w, parts[1])
+    own2_ref[...] = dot(w, parts[0]) + dot(w, parts[1])
     for n in range(LAYERS):
         v = y1_ref[n]
         o1_ref[n] = dot(q1_ref[n, 0], v) + dot(q1_ref[n, 1], v)
@@ -273,31 +273,47 @@
         passed[-1].start()
     for copy in passed:
         copy.wait_send()
+    for a, s, h in order:
+        part_of(a, s, h, 1 - c, rxq.at[a], s_qr, r_qr, partner).wait_recv()
+
+
+def finish(o1_ref, own2_ref, y2_ref, rxq, out1, out2, buf, sems):
+    x = lax.axis_index("layer")
+    head = lax.axis_index("head")
+    y, z = head // 8, (head // 2) % 4
+    b0, b1 = (x + z) % 2, (y + z) % 2
+    copies = [pltpu.make_async_copy(
+        own2_ref, out2.at[b0 + 2 * b1], sems.at[LAYERS])]
+    for n in range(LAYERS):
+        copies.append(pltpu.make_async_copy(o1_ref.at[n], out1.at[n], sems.at[n]))
+    for copy in copies:
+        copy.start()
+    lays = [(1 - b0) + 2 * b1, b0 + 2 * (1 - b1), (1 - b0) + 2 * (1 - b1)]
     for a in range(3):
-        for s in range(2):
-            for h in range(SHARES):
-                part_of(a, s, h, 1 - c, rxq.at[a], s_qr, r_qr, partner).wait_recv()
         w = y2_ref[lays[a]]
-        total = None
-        for k in range(2):
-            full = unpacked(rxq[a, k])
-            term = dot(w, full)
-            total = term if total is None else total + term
-        o2_ref[lays[a]] = total
+        buf[a] = dot(w, unpacked(rxq[a, 0])) + dot(w, unpacked(rxq[a, 1]))
+        copies.append(pltpu.make_async_copy(buf.at[a], out2.at[lays[a]], sems.at[LAYERS + 1 + a]))
+        copies[-1].start()
+    for copy in copies:
+        copy.wait()
 
 
 def shards(momentum, grad_one, grad_two):
     vmem = pl.BlockSpec(memory_space=pltpu.VMEM)
     hbm = pl.BlockSpec(memory_space=pltpu.MemorySpace.HBM)
     dma = pltpu.SemaphoreType.DMA
-    return pl.pallas_call(
+    given = pl.pallas_call(
         exchange,
-        out_shape=(jax.ShapeDtypeStruct((LAYERS, ROWS, LATENT), f32),) * 2,
+        out_shape=(
+            jax.ShapeDtypeStruct((LAYERS, ROWS, LATENT), f32),
+            jax.ShapeDtypeStruct((ROWS, LATENT), f32),
+            jax.ShapeDtypeStruct((LAYERS, ROWS, LATENT), bf16),
+            jax.ShapeDtypeStruct((3, 2, 2 * HALF, T), bf16),
+        ),
         in_specs=[hbm] * 3,
-        out_specs=(vmem,) * 2,
+        out_specs=(vmem,) * 4,
         scratch_shapes=[
             pltpu.VMEM((3, LAYERS, ROWS, LATENT), bf16),
-            pltpu.VMEM((LAYERS, ROWS, LATENT), bf16),
             pltpu.VMEM((LAYERS, ROWS, LATENT), bf16),
             pltpu.VMEM((LAYERS, 2, ROWS, ROWS), bf16),
             pltpu.VMEM((6, 128, LATENT), bf16),
@@ -307,15 +323,26 @@
             pltpu.VMEM((15, PIECE, T), f32),
             pltpu.VMEM((2 * HALF, T), f32),
             pltpu.VMEM((2, 2 * HALF, T), bf16),
-            pltpu.VMEM((3, 2, 2 * HALF, T), bf16),
             dma((3, LAYERS)), dma((6,)), dma((6,)), dma, dma,
             dma((15,)), dma((15,)), dma((15,)), dma((15,)), dma((16,)), dma((16,)),
             dma((3, 2, SHARES)), dma((3, 2, SHARES)), dma((3, 2, SHARES)), dma((3, 2, SHARES)),
         ],
         compiler_params=pltpu.CompilerParams(
-            collective_id=0, has_side_effects=True, vmem_limit_bytes=59 << 20),
+            collective_id=0, has_side_effects=True, vmem_limit_bytes=32 << 20),
         name="exchange",
-    )(momentum, grad_one, grad_two)
+    )(*[
+        pltpu.with_memory_space_constraint(v, pltpu.MemorySpace.HBM)
+        for v in (momentum, grad_one, grad_two)
+    ])
+    return pl.pallas_call(
+        finish,
+        out_shape=(jax.ShapeDtypeStruct((LAYERS, ROWS, LATENT), f32),) * 2,
+        in_specs=[vmem] * 4,
+        out_specs=(hbm,) * 2,
+        scratch_shapes=[pltpu.VMEM((3, ROWS, LATENT), f32), dma((LAYERS + 4,))],
+        compiler_params=pltpu.CompilerParams(vmem_limit_bytes=12 << 20),
+        name="finish",
+    )(*given)
 
 
 def solution(mesh):

time: 74.2 us -> 69 us (0.930)
  local copies, waits for them, and re-layouts: 4.55 us -> 0 us
  Pallas kernels: 68.9 us -> 68.1 us
    unnamed x4 -> x0, local copies, waits for them, and re-layouts: 4.55 us -> none
    pallas_call x1, Pallas kernels: 68.9 us -> 66 us  [shards(): pl.pallas_call(exchange, out_shape=(jax.ShapeDtypeStruct((LAYERS, ROWS, L...]
    pallas_call x0 -> x1, Pallas kernels: none -> 2.1 us  [shards(): pl.pallas_call(finish, out_shape=(jax.ShapeDtypeStruct((LAYERS, ROWS, LAT...]
where the time goes in v4:
time: 69 us; the launch traced here: 68.9 us
  Pallas kernels  68.1 us (99%)
  between operations  0.8 us (1%)
    pallas_call x1, Pallas kernels, shards(): pl.pallas_call(exchange, out_shape=(jax.ShapeDtypeStruct((LAYERS, ROWS, L...  66 us
    pallas_call x1, Pallas kernels, shards(): pl.pallas_call(finish, out_shape=(jax.ShapeDtypeStruct((LAYERS, ROWS, LAT...  2.1 us

profile of v4, /device:TPU:1, one launch (start us, length us, event | category | flops | bytes accessed | tf_op | source)
XLA Modules:
  0.0 68.9 jit_solution(9681792070132066231)
XLA Ops:
  0.6 66.0 %exchange.1 = (f32[4,256,512]{2,1,0:T(8,128)S(1)}, f32[256,512]{1,0:T(8,128)S(1)}, bf16[4,256,512]{2,1,0:T(8,128)(2,1)S(1)}, bf16[3,2,1280,128]{3,2,1,0:T(8,128)(2,1)S(1)}) custom-call(bf16[4,256,512]{2,1,0:T(8,128)(2,1)} %m_hbm.1, bf16[4,256,512]{2,1,0:T(8,128)(2,1)} %g1_hbm.1, bf16[4,256,512]{2,1,0:T(8,128)(2,1)} %g2_hbm.1), custom_call_target="tpu_custom_call" | custom-call | tf_op jit(solution)/shard_map/exchange/pallas_call | solution.py:305
  66.6 2.1 %finish.1 = (f32[4,256,512]{2,1,0:T(8,128)}, f32[4,256,512]{2,1,0:T(8,128)}) custom-call(f32[4,256,512]{2,1,0:T(8,128)S(1)} %get-tuple-element.6.o1_ref, f32[256,512]{1,0:T(8,128)S(1)} %get-tuple-element.7.own2_ref, bf16[4,256,512]{2,1,0:T(8,128)(2,1)S(1)} %get-tuple-element.8.y2_ref, bf16[3,2,1280,128]{3,2,1,0:T(8,128)(2,1)S(1)} %get-tuple-element.9.rxq), custom_call_target="tpu_custom_call" | custom-call | tf_op jit(solution)/shard_map/finish/pallas_call | solution.py:337

commit v5 on v4

--- a/solution.py
+++ b/solution.py
@@ -95,7 +95,7 @@
 
 def exchange(
     m_hbm, g1_hbm, g2_hbm, o1_ref, own2_ref, y2_ref, rxq,
-    ins, y1_ref, q1_ref, rx, part, core_in, own, rs, gath, packed,
+    ins, y1_ref, q1_ref, rx, part, core_in, own, rs, gath, packed, q2_ref,
     s_in, s_row, r_row, s_core, r_core, s_rs, r_rs, s_ag, r_ag, s_rel, r_rel,
     s_q, r_q, s_qr, r_qr,
 ):
@@ -123,6 +123,7 @@
         team.append(((2 * i2 + (b0 + z2) % 2, 2 * j2 + (b1 + z2) % 2, z2),
                      (i2 * 2 + j2) * 4 + z2))
     partner = at(x, y, z, 1 - c)
+    always = x < 4
 
     loads = [
         [pltpu.make_async_copy(h.at[n], ins.at[k, n], s_in.at[k, n])
@@ -139,12 +140,14 @@
     for who in greet:
         pl.semaphore_signal(barrier, inc=1, device_id=who, device_id_type=MESH)
 
-    for n in range(LAYERS):
-        for copy in loads[n]:
-            copy.wait()
-        one = (momentum_decay * ins[0, n].astype(f32) + ins[1, n].astype(f32)).astype(bf16)
-        y1_ref[n] = one
-        y2_ref[n] = (momentum_decay * one.astype(f32) + ins[2, n].astype(f32)).astype(bf16)
+    @pl.when(always)
+    def _():
+        for n in range(LAYERS):
+            for copy in loads[n]:
+                copy.wait()
+            one = (momentum_decay * ins[0, n].astype(f32) + ins[1, n].astype(f32)).astype(bf16)
+            y1_ref[n] = one
+            y2_ref[n] = (momentum_decay * one.astype(f32) + ins[2, n].astype(f32)).astype(bf16)
 
     pl.semaphore_wait(barrier, len(greet))
 
@@ -175,8 +178,10 @@
             q1_ref[n, 0] = high
             q1_ref[n, 1] = low
 
-    for copy in row_copies:
-        copy.wait()
+    @pl.when(always)
+    def _():
+        for copy in row_copies:
+            copy.wait()
 
     def gram_rows(i):
         total = None
@@ -187,11 +192,13 @@
             total = g if total is None else total + g
         return total
 
-    for i4 in range(4):
-        g = gram_rows(i4)
-        for j4 in range(i4, 4):
-            b = BLOCKS.index((i4, j4))
-            part[pl.ds(b * T, T), :] = g[:, (j4 - i4) * T:(j4 - i4 + 1) * T]
+    @pl.when(always)
+    def _():
+        for i4 in range(4):
+            g = gram_rows(i4)
+            for j4 in range(i4, 4):
+                b = BLOCKS.index((i4, j4))
+                part[pl.ds(b * T, T), :] = g[:, (j4 - i4) * T:(j4 - i4 + 1) * T]
 
     theirs = pl.ds(pl.multiple_of((1 - c) * HALF, 8), HALF)
     mine = pl.ds(pl.multiple_of(c * HALF, 8), HALF)
@@ -207,7 +214,10 @@
             s_rs.at[k], r_rs.at[k], at(*p, c)))
     for copy in rs_copies:
         copy.start()
-    heads((0, 1))
+    @pl.when(always)
+    def _():
+        heads((0, 1))
+
     for copy in rs_copies:
         copy.wait()
     total = own[pl.ds(pl.multiple_of(t * PIECE, 8), PIECE), :]
@@ -221,7 +231,9 @@
     ]
     for copy in ag_copies:
         copy.start()
-    heads((2, 3))
+    @pl.when(always)
+    def _():
+        heads((2, 3))
 
     def relay(k, t3, core):
         there = pl.ds(pl.multiple_of(core * HALF + t3 * PIECE, 8), PIECE)
@@ -243,13 +255,17 @@
     for k, t3 in relays:
         relay(k, t3, 1 - c).wait_recv()
 
-    gram = unpacked(gath[...])
-    norm = jnp.sqrt(trace(gram)) + norm_epsilon
-    q = polynomials([gram * (1.0 / (norm * norm))], mm_even)[0]
-    parts = split(q * (math.sqrt(ALL_ROWS) / norm))
-    for k in range(2):
-        for b, (bi, bj) in enumerate(BLOCKS):
-            packed[k, b * T:(b + 1) * T, :] = parts[k][bi * T:(bi + 1) * T, bj * T:(bj + 1) * T]
+    @pl.when(always)
+    def _():
+        gram = unpacked(gath[...])
+        norm = jnp.sqrt(trace(gram)) + norm_epsilon
+        q = polynomials([gram * (1.0 / (norm * norm))], mm_even)[0]
+        parts = split(q * (math.sqrt(ALL_ROWS) / norm))
+        for k in range(2):
+            q2_ref[k] = parts[k]
+            for b, (bi, bj) in enumerate(BLOCKS):
+                packed[k, b * T:(b + 1) * T, :] = parts[k][
+                    bi * T:(bi + 1) * T, bj * T:(bj + 1) * T]
 
     def part_of(a, s, h, core, src, ss, rr, who):
         rows = pl.ds(pl.multiple_of((s * 2 + core) * QUARTER + h * SHARE, 16), SHARE)
@@ -261,11 +277,14 @@
     ]
     for copy in q_copies:
         copy.start()
-    w = y2_ref[lay]
-    own2_ref[...] = dot(w, parts[0]) + dot(w, parts[1])
-    for n in range(LAYERS):
-        v = y1_ref[n]
-        o1_ref[n] = dot(q1_ref[n, 0], v) + dot(q1_ref[n, 1], v)
+    @pl.when(always)
+    def _():
+        w = y2_ref[lay]
+        own2_ref[...] = dot(w, q2_ref[0]) + dot(w, q2_ref[1])
+        for n in range(LAYERS):
+            v = y1_ref[n]
+            o1_ref[n] = dot(q1_ref[n, 0], v) + dot(q1_ref[n, 1], v)
+
     passed = []
     for copy, (a, s, h) in zip(q_copies, order):
         copy.wait()
@@ -323,6 +342,7 @@
             pltpu.VMEM((15, PIECE, T), f32),
             pltpu.VMEM((2 * HALF, T), f32),
             pltpu.VMEM((2, 2 * HALF, T), bf16),
+            pltpu.VMEM((2, LATENT, LATENT), bf16),
             dma((3, LAYERS)), dma((6,)), dma((6,)), dma, dma,
             dma((15,)), dma((15,)), dma((15,)), dma((15,)), dma((16,)), dma((16,)),
             dma((3, 2, SHARES)), dma((3, 2, SHARES)), dma((3, 2, SHARES)), dma((3, 2, SHARES)),

time: 69 us -> 58.8 us (0.85)
  Pallas kernels: 68.1 us -> 57.9 us
    pallas_call x1, Pallas kernels: 66 us -> 55.8 us  [shards(): pl.pallas_call(exchange, out_shape=(jax.ShapeDtypeStruct((LAYERS, ROWS, L...]
where the time goes in v5:
time: 58.8 us; the launch traced here: 58.7 us
  Pallas kernels  57.9 us (98%)
  between operations  0.8 us (1%)
    pallas_call x1, Pallas kernels, shards(): pl.pallas_call(exchange, out_shape=(jax.ShapeDtypeStruct((LAYERS, ROWS, L...  55.8 us
    pallas_call x1, Pallas kernels, shards(): pl.pallas_call(finish, out_shape=(jax.ShapeDtypeStruct((LAYERS, ROWS, LAT...  2.1 us

profile of v5, /device:TPU:1, one launch (start us, length us, event | category | flops | bytes accessed | tf_op | source)
XLA Modules:
  0.0 58.7 jit_solution(7322566064046830803)
XLA Ops:
  0.6 55.8 %exchange.1 = (f32[4,256,512]{2,1,0:T(8,128)S(1)}, f32[256,512]{1,0:T(8,128)S(1)}, bf16[4,256,512]{2,1,0:T(8,128)(2,1)S(1)}, bf16[3,2,1280,128]{3,2,1,0:T(8,128)(2,1)S(1)}) custom-call(bf16[4,256,512]{2,1,0:T(8,128)(2,1)} %m_hbm.1, bf16[4,256,512]{2,1,0:T(8,128)(2,1)} %g1_hbm.1, bf16[4,256,512]{2,1,0:T(8,128)(2,1)} %g2_hbm.1), custom_call_target="tpu_custom_call" | custom-call | tf_op jit(solution)/shard_map/exchange/pallas_call | solution.py:324
  56.5 2.1 %finish.1 = (f32[4,256,512]{2,1,0:T(8,128)}, f32[4,256,512]{2,1,0:T(8,128)}) custom-call(f32[4,256,512]{2,1,0:T(8,128)S(1)} %get-tuple-element.6.o1_ref, f32[256,512]{1,0:T(8,128)S(1)} %get-tuple-element.7.own2_ref, bf16[4,256,512]{2,1,0:T(8,128)(2,1)S(1)} %get-tuple-element.8.y2_ref, bf16[3,2,1280,128]{3,2,1,0:T(8,128)(2,1)S(1)} %get-tuple-element.9.rxq), custom_call_target="tpu_custom_call" | custom-call | tf_op jit(solution)/shard_map/finish/pallas_call | solution.py:357

commit v6 on v5

v6 whole, which is shorter than its diff:
```python
import functools
import math

import jax
import jax.numpy as jnp
from jax import lax
from jax.experimental import pallas as pl
from jax.experimental.pallas import tpu as pltpu
from jax.sharding import PartitionSpec as P

NS_ITERS = 5
quintic_a = 3.4445
quintic_b = -4.775
quintic_c = 2.0315
norm_epsilon = 1e-07
momentum_decay = 0.95

bf16 = jnp.bfloat16
f32 = jnp.float32
MESH = pl.DeviceIdType.MESH
LAYERS, ROWS, LATENT = 4, 256, 512
ALL_ROWS = 32768
T = 128
BLOCKS = [(i, j) for i in range(4) for j in range(i, 4)]
SENT = [(0, 0), (0, 1), (1, 1), (0, 2), (0, 3), (2, 2), (2, 3), (3, 3), (2, 1), (3, 1)]
HALF = len(BLOCKS) * T // 2
PIECE = HALF // 16
QUARTER = HALF // 2
SHARES = 4
CHUNK = 64
SHARE = QUARTER // SHARES
OFFSETS = [(1, 1, 2), (1, 1, 0), (1, 0, 2), (0, 1, 2)]
OFFSETS += [(i, j, z) for z in (1, 3) for i in (0, 1) for j in (0, 1)]
OFFSETS += [(1, 0, 0), (0, 1, 0), (0, 0, 2)]


def split(x):
    high = x.astype(bf16)
    return high, (x - high.astype(f32)).astype(bf16)


def dot(x, y):
    return jnp.dot(x, y, preferred_element_type=f32)


def dot3(x, y):
    return dot(x[0], y[0]) + (dot(x[0], y[1]) + dot(x[1], y[0]))


def mm(x, y):
    return dot3(x, y)


def mm_even(x, y):
    h = x[0].shape[0] // 2
    top = dot3([t[:h] for t in x], y)
    low = dot3([t[h:] for t in x], [t[:, h:] for t in y])
    return jnp.concatenate([top, jnp.concatenate([top[:, h:].T, low], 1)], 0)


def square(x):
    high, low = x
    cross = dot(high, low)
    return dot(high, high) + (cross + cross.T)


def square_even(x):
    high, low = x
    h = high.shape[0] // 2
    cross = dot(high, low)
    top, last = dot(high[:h], high), dot(high[h:], high[:, h:])
    first = top[:, :h] + (cross[:h, :h] + cross[:h, :h].T)
    side = top[:, h:] + (cross[:h, h:] + cross[h:, :h].T)
    last = last + (cross[h:, h:] + cross[h:, h:].T)
    return jnp.concatenate(
        [jnp.concatenate([first, side], 1), jnp.concatenate([side.T, last], 1)], 0)


def eye(n):
    rows = lax.broadcasted_iota(jnp.int32, (n, n), 0)
    return rows == lax.broadcasted_iota(jnp.int32, (n, n), 1)


def half_polynomial(gram, product, scratch, start):
    n = gram.shape[0]
    diag = jnp.where(eye(n), f32(quintic_a), f32(0.0))
    s, q = gram, None
    for k in range(NS_ITERS):
        part = split(s)
        m = diag + (quintic_b * s + quintic_c * square_even(part))
        if k == 0:
            scratch[...] = m
        ms = split(m)
        if k < NS_ITERS - 1:
            s = product(split(product(part, ms)), ms)
        q = scratch[pl.ds(start, n // 2), :] if k == 0 else dot3(split(q), ms)
    return q


def polynomials(grams, product):
    n = grams[0].shape[0]
    diag = jnp.where(eye(n), f32(quintic_a), f32(0.0))
    s, q = list(grams), [None] * len(grams)
    for k in range(NS_ITERS):
        parts = [split(t) for t in s]
        m = [
            diag + (quintic_b * t + quintic_c * square(u)) for t, u in zip(s, parts)
        ]
        ms = [split(t) for t in m]
        if k < NS_ITERS - 1:
            r = [split(product(u, v)) for u, v in zip(parts, ms)]
            s = [product(u, v) for u, v in zip(r, ms)]
        q = m if k == 0 else [product(split(u), v) for u, v in zip(q, ms)]
    return q


def unpacked(blocks, order=BLOCKS):
    tiles = {}
    for b, (i, j) in enumerate(order):
        v = blocks[b * T:(b + 1) * T, :]
        tiles[i, j] = v
        if i != j:
            tiles[j, i] = v.T
    return jnp.concatenate(
        [jnp.concatenate([tiles[i, j] for j in range(4)], 1) for i in range(4)], 0)


def restored(blocks):
    return unpacked(blocks, SENT)


def trace(x):
    return jnp.sum(jnp.where(eye(x.shape[0]), x, f32(0.0)))


def exchange(
    m_hbm, g1_hbm, g2_hbm, o1_ref, own2_ref, y2_ref, rxq,
    ins, y1_ref, q1_ref, rx, part, core_in, own, rs, gath, q_full, q_half, rounds,
    s_in, s_row, r_row, s_core, r_core, s_rs, r_rs, s_ag, r_ag, s_rel, r_rel,
    s_q, r_q, s_qr, r_qr, s_own, r_own,
):
    x = lax.axis_index("layer")
    head = lax.axis_index("head")
    y, z, c = head // 8, (head // 2) % 4, head % 2
    b0, b1 = (x + z) % 2, (y + z) % 2
    lay = b0 + 2 * b1
    lays = [(1 - b0) + 2 * b1, b0 + 2 * (1 - b1), (1 - b0) + 2 * (1 - b1)]
    i, j = x // 2, y // 2
    t = (i * 2 + j) * 4 + z

    def at(x, y, z, c):
        return (x, (y * 4 + z) * 2 + c)

    steps = []
    for a in range(3):
        for s in range(2):
            d = 1 if s == 0 else 3
            steps.append(((x + d) % 4 if a == 0 else x, (y + d) % 4 if a == 1 else y,
                          (z + d) % 4 if a == 2 else z))
    team = []
    for di, dj, dz in OFFSETS:
        i2, j2, z2 = (i + di) % 2, (j + dj) % 2, (z + dz) % 4
        team.append(((2 * i2 + (b0 + z2) % 2, 2 * j2 + (b1 + z2) % 2, z2),
                     (i2 * 2 + j2) * 4 + z2))
    partner = at(x, y, z, 1 - c)
    always = x < 4

    def phase(name):
        def run(body):
            with jax.named_scope(name):
                pl.when(always)(body)
        return run


    barrier = pltpu.get_barrier_semaphore()
    greet = [partner]
    greet += [at(*p, c) for p in steps]
    for who in greet:
        pl.semaphore_signal(barrier, inc=1, device_id=who, device_id_type=MESH)

    turn = lays + [lay]
    loads = [
        [pltpu.make_async_copy(h.at[n], ins.at[k, w], s_in.at[k, w])
         for k, h in enumerate((m_hbm, g1_hbm, g2_hbm))]
        for w, n in enumerate(turn)
    ]
    for group in loads:
        for copy in group:
            copy.start()
    def send(src, dst, ss, rr, who):
        return pltpu.make_async_remote_copy(
            src_ref=src, dst_ref=dst, send_sem=ss, recv_sem=rr, device_id=who,
            device_id_type=MESH)

    row_copies = [
        [send(y2_ref.at[lays[k // 2], pl.ds((k % 2) * 128 + h * CHUNK, CHUNK), :],
              rx.at[h, pl.ds(k * CHUNK, CHUNK), :], s_row.at[h, k], r_row.at[h, k], at(*p, c))
         for k, p in enumerate(steps)]
        for h in range(2)
    ]

    near = [at(*p, c) for p in steps]
    far = [at((x + 2) % 4, y, z, c), at(x, (y + 2) % 4, z, c), at(x, y, (z + 2) % 4, c)]
    told = [near, near + far, far[:1]]

    def tell(k):
        for who in told[k]:
            pl.semaphore_signal(rounds.at[k], inc=1, device_id=who, device_id_type=MESH)

    @phase("w_barrier")
    def _():
        pl.semaphore_wait(barrier, len(greet))
        tell(0)

    for w, n in enumerate(turn):
        @phase("p01")
        def _(w=w, n=n):
            for copy in loads[w]:
                copy.wait()
            one = (momentum_decay * ins[0, w].astype(f32) + ins[1, w].astype(f32)).astype(bf16)
            y1_ref[n] = one
            y2_ref[n] = (momentum_decay * one.astype(f32) + ins[2, w].astype(f32)).astype(bf16)

        if w == 0:
            @phase("w_tell")
            def _():
                pl.semaphore_wait(rounds.at[0], len(told[0]))
                tell(1)
        if w < 3:
            for h in range(2):
                for k in (2 * w, 2 * w + 1):
                    row_copies[h][k].start()

    @phase("w_rounds")
    def _():
        pl.semaphore_wait(rounds.at[1], len(told[1]))
        tell(2)

    def heads(ns):
        grams = []
        norms = []
        for n in ns:
            v = y1_ref[n]
            g = lax.dot_general(v, v, (((1,), (1,)), ((), ())), preferred_element_type=f32)
            norm = jnp.sqrt(trace(g)) + norm_epsilon
            grams.append(g * (1.0 / (norm * norm)))
            norms.append(norm)
        for n, q, norm in zip(ns, polynomials(grams, mm), norms):
            high, low = split(q * (math.sqrt(max(ROWS, LATENT)) / norm))
            q1_ref[n, 0] = high
            q1_ref[n, 1] = low

    def gram_of(views, first):
        for i4 in range(4):
            total = None
            for v in views:
                g = lax.dot_general(
                    v[:, pl.ds(i4 * T, T)], v[:, pl.ds(i4 * T, LATENT - i4 * T)],
                    (((0,), (0,)), ((), ())), preferred_element_type=f32)
                total = g if total is None else total + g
            for j4 in range(i4, 4):
                rows = pl.ds(BLOCKS.index((i4, j4)) * T, T)
                value = total[:, (j4 - i4) * T:(j4 - i4 + 1) * T]
                part[rows, :] = value if first else part[rows, :] + value

    @phase("w_rows0")
    def _():
        for copy in row_copies[0]:
            copy.wait()

    @phase("p02")
    def _():
        gram_of([y2_ref.at[lay], rx.at[0]], True)

    @phase("w_rows1")
    def _():
        for copy in row_copies[1]:
            copy.wait()

    @phase("p03")
    def _():
        gram_of([rx.at[1]], False)

    theirs = pl.ds(pl.multiple_of((1 - c) * HALF, 8), HALF)
    mine = pl.ds(pl.multiple_of(c * HALF, 8), HALF)
    swap = send(part.at[theirs, :], core_in, s_core, r_core, partner)
    swap.start()
    @phase("w_swap")
    def _():
        swap.wait()
        own[...] = part[mine, :] + core_in[...]

    rs_copies = []
    for k, (p, t2) in enumerate(team):
        rs_copies.append(send(
            own.at[pl.ds(pl.multiple_of(t2 * PIECE, 8), PIECE), :], rs.at[k],
            s_rs.at[k], r_rs.at[k], at(*p, c)))
    pl.semaphore_wait(rounds.at[2], len(told[2]))
    for copy in rs_copies:
        copy.start()
    @phase("p04")
    def _():
        heads((0, 1))

    @phase("w_rs")
    def _():
        for copy in rs_copies:
            copy.wait()

    total = own[pl.ds(pl.multiple_of(t * PIECE, 8), PIECE), :]
    for k in range(15):
        total = total + rs[k]
    here = pl.ds(pl.multiple_of(c * HALF + t * PIECE, 8), PIECE)
    gath[here, :] = total
    ag_copies = [
        send(gath.at[here, :], gath.at[here, :], s_ag.at[k], r_ag.at[k], at(*p, c))
        for k, (p, _) in enumerate(team)
    ]
    for copy in ag_copies:
        copy.start()
    @phase("p05")
    def _():
        heads((2, 3))

    def relay(k, t3, core):
        there = pl.ds(pl.multiple_of(core * HALF + t3 * PIECE, 8), PIECE)
        return send(gath.at[there, :], gath.at[there, :], s_rel.at[k], r_rel.at[k], partner)

    relays = [(15, t)]
    for k, (di, dj, dz) in enumerate(OFFSETS):
        relays.append((k, (((i + di) % 2) * 2 + (j + dj) % 2) * 4 + (z + 4 - dz) % 4))
    @phase("w_ag")
    def _():
        for k, t3 in [relays[0]] + relays[:0:-1]:
            if k < 15:
                there = pl.ds(pl.multiple_of(c * HALF + t3 * PIECE, 8), PIECE)
                send(gath.at[there, :], gath.at[there, :], s_ag.at[k], r_ag.at[k],
                     at(*team[k][0], c)).wait_recv()
            relay(k, t3, c).start()

    @phase("w_relay")
    def _():
        for copy in ag_copies:
            copy.wait_send()
        for k, t3 in relays:
            relay(k, t3, c).wait_send()
        for k, t3 in relays:
            relay(k, t3, 1 - c).wait_recv()

    @phase("p06")
    def _():
        gram = unpacked(gath[...])
        norm = jnp.sqrt(trace(gram)) + norm_epsilon
        q = half_polynomial(
            gram * (1.0 / (norm * norm)), mm_even, q_full, pl.multiple_of(c * 256, 256))
        parts = split(q * (math.sqrt(ALL_ROWS) / norm))
        for k in range(2):
            q_half[k] = parts[k]
            where = [(0, 256 * c), (0, 256 * c + T), (T, 256 * c + T), (0, 256 - T * c),
                     (T * c, 384 - 256 * c)]
            for b, (row, column) in enumerate(where):
                tile = q_half[k, pl.ds(pl.multiple_of(row, T), T),
                              pl.ds(pl.multiple_of(column, T), T)]
                rxq[3, k, pl.ds(pl.multiple_of(c * HALF + b * T, T), T), :] = tile

    def part_of(a, s, h, core, src, ss, rr, who):
        rows = pl.ds(pl.multiple_of(core * HALF + s * QUARTER + h * SHARE, 16), SHARE)
        return send(rxq.at[src, :, rows, :], rxq.at[a, :, rows, :], ss.at[a, s, h],
                    rr.at[a, s, h], who)

    order = [(a, s, h) for h in range(SHARES) for a in range(3) for s in range(2)]
    q_copies = [part_of(a, s, h, c, 3, s_q, r_q, at(*steps[2 * a + s], c)) for a, s, h in order]
    for copy in q_copies:
        copy.start()
    own_half = [send(rxq.at[3, :, rows, :], rxq.at[3, :, rows, :], s_own, r_own, partner)
                for rows in (mine, theirs)]
    own_half[0].start()

    @phase("p07")
    def _():
        for n in range(LAYERS):
            v = y1_ref[n]
            o1_ref[n] = dot(q1_ref[n, 0], v) + dot(q1_ref[n, 1], v)

    @phase("w_ownhalf")
    def _():
        own_half[0].wait_send()
        own_half[1].wait_recv()

    @phase("p08")
    def _():
        w = y2_ref[lay]
        own2_ref[...] = dot(w, restored(rxq[3, 0])) + dot(w, restored(rxq[3, 1]))

    passed = [part_of(a, s, h, c, a, s_qr, r_qr, partner) for a, s, h in order]

    @phase("w_q")
    def _():
        for copy, onward in zip(q_copies, passed):
            copy.wait()
            onward.start()

    @phase("w_final")
    def _():
        for copy in passed:
            copy.wait_send()
        for a, s, h in order:
            part_of(a, s, h, 1 - c, a, s_qr, r_qr, partner).wait_recv()

def finish(o1_ref, own2_ref, y2_ref, rxq, out1, out2, buf, sems):
    x = lax.axis_index("layer")
    head = lax.axis_index("head")
    y, z = head // 8, (head // 2) % 4
    b0, b1 = (x + z) % 2, (y + z) % 2
    copies = [pltpu.make_async_copy(
        own2_ref, out2.at[b0 + 2 * b1], sems.at[LAYERS])]
    for n in range(LAYERS):
        copies.append(pltpu.make_async_copy(o1_ref.at[n], out1.at[n], sems.at[n]))
    for copy in copies:
        copy.start()
    lays = [(1 - b0) + 2 * b1, b0 + 2 * (1 - b1), (1 - b0) + 2 * (1 - b1)]
    for a in range(3):
        w = y2_ref[lays[a]]
        buf[a] = dot(w, restored(rxq[a, 0])) + dot(w, restored(rxq[a, 1]))
        copies.append(pltpu.make_async_copy(buf.at[a], out2.at[lays[a]], sems.at[LAYERS + 1 + a]))
        copies[-1].start()
    for copy in copies:
        copy.wait()


def shards(momentum, grad_one, grad_two):
    vmem = pl.BlockSpec(memory_space=pltpu.VMEM)
    hbm = pl.BlockSpec(memory_space=pltpu.MemorySpace.HBM)
    dma = pltpu.SemaphoreType.DMA
    given = pl.pallas_call(
        exchange,
        out_shape=(
            jax.ShapeDtypeStruct((LAYERS, ROWS, LATENT), f32),
            jax.ShapeDtypeStruct((ROWS, LATENT), f32),
            jax.ShapeDtypeStruct((LAYERS, ROWS, LATENT), bf16),
            jax.ShapeDtypeStruct((4, 2, 2 * HALF, T), bf16),
        ),
        in_specs=[hbm] * 3,
        out_specs=(vmem,) * 4,
        scratch_shapes=[
            pltpu.VMEM((3, LAYERS, ROWS, LATENT), bf16),
            pltpu.VMEM((LAYERS, ROWS, LATENT), bf16),
            pltpu.VMEM((LAYERS, 2, ROWS, ROWS), bf16),
            pltpu.VMEM((2, 6 * CHUNK, LATENT), bf16),
            pltpu.VMEM((2 * HALF, T), f32),
            pltpu.VMEM((HALF, T), f32),
            pltpu.VMEM((HALF, T), f32),
            pltpu.VMEM((15, PIECE, T), f32),
            pltpu.VMEM((2 * HALF, T), f32),
            pltpu.VMEM((LATENT, LATENT), f32),
            pltpu.VMEM((2, LATENT // 2, LATENT), bf16),
            pltpu.SemaphoreType.REGULAR((3,)),
            dma((3, LAYERS)), dma((2, 6)), dma((2, 6)), dma, dma,
            dma((15,)), dma((15,)), dma((15,)), dma((15,)), dma((16,)), dma((16,)),
            dma((3, 2, SHARES)), dma((3, 2, SHARES)), dma((3, 2, SHARES)), dma((3, 2, SHARES)),
            dma, dma,
        ],
        compiler_params=pltpu.CompilerParams(
            collective_id=0, has_side_effects=True, vmem_limit_bytes=32 << 20),
        name="exchange",
    )(*[
        pltpu.with_memory_space_constraint(v, pltpu.MemorySpace.HBM)
        for v in (momentum, grad_one, grad_two)
    ])
    return pl.pallas_call(
        finish,
        out_shape=(jax.ShapeDtypeStruct((LAYERS, ROWS, LATENT), f32),) * 2,
        in_specs=[vmem] * 4,
        out_specs=(hbm,) * 2,
        scratch_shapes=[pltpu.VMEM((3, ROWS, LATENT), f32), dma((LAYERS + 4,))],
        compiler_params=pltpu.CompilerParams(vmem_limit_bytes=12 << 20),
        name="finish",
    )(*given)


def solution(mesh):
    spec = P(None, ("layer", "head"), None)
    return jax.shard_map(
        shards, mesh=mesh, in_specs=(spec,) * 3, out_specs=(spec,) * 2, check_vma=False
    )
```

time: 58.8 us -> 55.5 us (0.944)
  Pallas kernels: 57.9 us -> 54.6 us
    pallas_call x1, Pallas kernels: 55.8 us -> 52.5 us  [shards(): pl.pallas_call(exchange, out_shape=(jax.ShapeDtypeStruct((LAYERS, ROWS, L...]
where the time goes in v6:
time: 55.5 us; the launch traced here: 55.4 us
  Pallas kernels  54.6 us (98%)
  between operations  0.8 us (1%)
    pallas_call x1, Pallas kernels, shards(): pl.pallas_call(exchange, out_shape=(jax.ShapeDtypeStruct((LAYERS, ROWS, L...  52.5 us
    pallas_call x1, Pallas kernels, shards(): pl.pallas_call(finish, out_shape=(jax.ShapeDtypeStruct((LAYERS, ROWS, LAT...  2.1 us

profile of v6, /device:TPU:1, one launch (start us, length us, event | category | flops | bytes accessed | tf_op | source)
XLA Modules:
  0.0 55.4 jit_solution(17413899676759304199)
XLA Ops:
  0.6 52.5 %exchange.1 = (f32[4,256,512]{2,1,0:T(8,128)S(1)}, f32[256,512]{1,0:T(8,128)S(1)}, bf16[4,256,512]{2,1,0:T(8,128)(2,1)S(1)}, bf16[4,2,1280,128]{3,2,1,0:T(8,128)(2,1)S(1)}) custom-call(bf16[4,256,512]{2,1,0:T(8,128)(2,1)} %m_hbm.1, bf16[4,256,512]{2,1,0:T(8,128)(2,1)} %g1_hbm.1, bf16[4,256,512]{2,1,0:T(8,128)(2,1)} %g2_hbm.1), custom_call_target="tpu_custom_call" | custom-call | tf_op jit(solution)/shard_map/exchange/pallas_call | solution.py:435
  53.2 2.1 %finish.1 = (f32[4,256,512]{2,1,0:T(8,128)}, f32[4,256,512]{2,1,0:T(8,128)}) custom-call(f32[4,256,512]{2,1,0:T(8,128)S(1)} %get-tuple-element.6.o1_ref, f32[256,512]{1,0:T(8,128)S(1)} %get-tuple-element.7.own2_ref, bf16[4,256,512]{2,1,0:T(8,128)(2,1)S(1)} %get-tuple-element.8.y2_ref, bf16[4,2,1280,128]{3,2,1,0:T(8,128)(2,1)S(1)} %get-tuple-element.9.rxq), custom_call_target="tpu_custom_call" | custom-call | tf_op jit(solution)/shard_map/finish/pallas_call | solution.py:470

commit v7 on v6

--- a/solution.py
+++ b/solution.py
@@ -22,13 +22,9 @@
 ALL_ROWS = 32768
 T = 128
 BLOCKS = [(i, j) for i in range(4) for j in range(i, 4)]
-SENT = [(0, 0), (0, 1), (1, 1), (0, 2), (0, 3), (2, 2), (2, 3), (3, 3), (2, 1), (3, 1)]
 HALF = len(BLOCKS) * T // 2
 PIECE = HALF // 16
-QUARTER = HALF // 2
-SHARES = 4
 CHUNK = 64
-SHARE = QUARTER // SHARES
 OFFSETS = [(1, 1, 2), (1, 1, 0), (1, 0, 2), (0, 1, 2)]
 OFFSETS += [(i, j, z) for z in (1, 3) for i in (0, 1) for j in (0, 1)]
 OFFSETS += [(1, 0, 0), (0, 1, 0), (0, 0, 2)]
@@ -56,12 +52,6 @@
     top = dot3([t[:h] for t in x], y)
     low = dot3([t[h:] for t in x], [t[:, h:] for t in y])
     return jnp.concatenate([top, jnp.concatenate([top[:, h:].T, low], 1)], 0)
-
-
-def square(x):
-    high, low = x
-    cross = dot(high, low)
-    return dot(high, high) + (cross + cross.T)
 
 
 def square_even(x):
@@ -81,19 +71,16 @@
     return rows == lax.broadcasted_iota(jnp.int32, (n, n), 1)
 
 
-def half_polynomial(gram, product, scratch, start):
-    n = gram.shape[0]
-    diag = jnp.where(eye(n), f32(quintic_a), f32(0.0))
+def layer_polynomial(gram):
+    diag = jnp.where(eye(gram.shape[0]), f32(quintic_a), f32(0.0))
     s, q = gram, None
     for k in range(NS_ITERS):
         part = split(s)
         m = diag + (quintic_b * s + quintic_c * square_even(part))
-        if k == 0:
-            scratch[...] = m
         ms = split(m)
         if k < NS_ITERS - 1:
-            s = product(split(product(part, ms)), ms)
-        q = scratch[pl.ds(start, n // 2), :] if k == 0 else dot3(split(q), ms)
+            s = mm_even(split(mm_even(part, ms)), ms)
+        q = m if k == 0 else mm_even(split(q), ms)
     return q
 
 
@@ -104,7 +91,7 @@
     for k in range(NS_ITERS):
         parts = [split(t) for t in s]
         m = [
-            diag + (quintic_b * t + quintic_c * square(u)) for t, u in zip(s, parts)
+            diag + (quintic_b * t + quintic_c * product(u, u)) for t, u in zip(s, parts)
         ]
         ms = [split(t) for t in m]
         if k < NS_ITERS - 1:
@@ -114,9 +101,9 @@
     return q
 
 
-def unpacked(blocks, order=BLOCKS):
+def unpacked(blocks):
     tiles = {}
-    for b, (i, j) in enumerate(order):
+    for b, (i, j) in enumerate(BLOCKS):
         v = blocks[b * T:(b + 1) * T, :]
         tiles[i, j] = v
         if i != j:
@@ -125,19 +112,15 @@
         [jnp.concatenate([tiles[i, j] for j in range(4)], 1) for i in range(4)], 0)
 
 
-def restored(blocks):
-    return unpacked(blocks, SENT)
-
-
 def trace(x):
     return jnp.sum(jnp.where(eye(x.shape[0]), x, f32(0.0)))
 
 
 def exchange(
-    m_hbm, g1_hbm, g2_hbm, o1_ref, own2_ref, y2_ref, rxq,
-    ins, y1_ref, q1_ref, rx, part, core_in, own, rs, gath, q_full, q_half, rounds,
+    m_hbm, g1_hbm, g2_hbm, o1_ref, own2_ref, got,
+    ins, y1_ref, y2_ref, q1_ref, rx, tx, part, core_in, own, rs, gath, q2_ref, rounds,
     s_in, s_row, r_row, s_core, r_core, s_rs, r_rs, s_ag, r_ag, s_rel, r_rel,
-    s_q, r_q, s_qr, r_qr, s_own, r_own,
+    s_q, r_q,
 ):
     x = lax.axis_index("layer")
     head = lax.axis_index("head")
@@ -351,63 +334,38 @@
     def _():
         gram = unpacked(gath[...])
         norm = jnp.sqrt(trace(gram)) + norm_epsilon
-        q = half_polynomial(
-            gram * (1.0 / (norm * norm)), mm_even, q_full, pl.multiple_of(c * 256, 256))
-        parts = split(q * (math.sqrt(ALL_ROWS) / norm))
-        for k in range(2):
-            q_half[k] = parts[k]
-            where = [(0, 256 * c), (0, 256 * c + T), (T, 256 * c + T), (0, 256 - T * c),
-                     (T * c, 384 - 256 * c)]
-            for b, (row, column) in enumerate(where):
-                tile = q_half[k, pl.ds(pl.multiple_of(row, T), T),
-                              pl.ds(pl.multiple_of(column, T), T)]
-                rxq[3, k, pl.ds(pl.multiple_of(c * HALF + b * T, T), T), :] = tile
-
-    def part_of(a, s, h, core, src, ss, rr, who):
-        rows = pl.ds(pl.multiple_of(core * HALF + s * QUARTER + h * SHARE, 16), SHARE)
-        return send(rxq.at[src, :, rows, :], rxq.at[a, :, rows, :], ss.at[a, s, h],
-                    rr.at[a, s, h], who)
-
-    order = [(a, s, h) for h in range(SHARES) for a in range(3) for s in range(2)]
-    q_copies = [part_of(a, s, h, c, 3, s_q, r_q, at(*steps[2 * a + s], c)) for a, s, h in order]
-    for copy in q_copies:
-        copy.start()
-    own_half = [send(rxq.at[3, :, rows, :], rxq.at[3, :, rows, :], s_own, r_own, partner)
-                for rows in (mine, theirs)]
-    own_half[0].start()
-
-    @phase("p07")
-    def _():
+        q = layer_polynomial(gram * (1.0 / (norm * norm)))
+        q2_ref[0], q2_ref[1] = split(q * (math.sqrt(ALL_ROWS) / norm))
+
+    back = []
+    for h in range(2):
+        @phase("p07")
+        def _(h=h):
+            w = rx[h]
+            tx[h] = (dot(w, q2_ref[0]) + dot(w, q2_ref[1])).astype(bf16)
+
+        for k, p in enumerate(steps):
+            back.append(send(
+                tx.at[h, pl.ds(k * CHUNK, CHUNK), :],
+                got.at[k // 2, pl.ds((k % 2) * 128 + h * CHUNK, CHUNK), :],
+                s_q.at[h, k], r_q.at[h, k], at(*steps[k ^ 1], c)))
+            back[-1].start()
+
+    @phase("p08")
+    def _():
+        w = y2_ref[lay]
+        own2_ref[...] = dot(w, q2_ref[0]) + dot(w, q2_ref[1])
         for n in range(LAYERS):
             v = y1_ref[n]
             o1_ref[n] = dot(q1_ref[n, 0], v) + dot(q1_ref[n, 1], v)
 
-    @phase("w_ownhalf")
-    def _():
-        own_half[0].wait_send()
-        own_half[1].wait_recv()
-
-    @phase("p08")
-    def _():
-        w = y2_ref[lay]
-        own2_ref[...] = dot(w, restored(rxq[3, 0])) + dot(w, restored(rxq[3, 1]))
-
-    passed = [part_of(a, s, h, c, a, s_qr, r_qr, partner) for a, s, h in order]
-
-    @phase("w_q")
-    def _():
-        for copy, onward in zip(q_copies, passed):
+    @phase("w_back")
+    def _():
+        for copy in back:
             copy.wait()
-            onward.start()
-
-    @phase("w_final")
-    def _():
-        for copy in passed:
-            copy.wait_send()
-        for a, s, h in order:
-            part_of(a, s, h, 1 - c, a, s_qr, r_qr, partner).wait_recv()
-
-def finish(o1_ref, own2_ref, y2_ref, rxq, out1, out2, buf, sems):
+
+
+def finish(o1_ref, own2_ref, got, out1, out2, buf, sems):
     x = lax.axis_index("layer")
     head = lax.axis_index("head")
     y, z = head // 8, (head // 2) % 4
@@ -420,8 +378,7 @@
         copy.start()
     lays = [(1 - b0) + 2 * b1, b0 + 2 * (1 - b1), (1 - b0) + 2 * (1 - b1)]
     for a in range(3):
-        w = y2_ref[lays[a]]
-        buf[a] = dot(w, restored(rxq[a, 0])) + dot(w, restored(rxq[a, 1]))
+        buf[a] = got[a].astype(f32)
         copies.append(pltpu.make_async_copy(buf.at[a], out2.at[lays[a]], sems.at[LAYERS + 1 + a]))
         copies[-1].start()
     for copy in copies:
@@ -437,28 +394,27 @@
         out_shape=(
             jax.ShapeDtypeStruct((LAYERS, ROWS, LATENT), f32),
             jax.ShapeDtypeStruct((ROWS, LATENT), f32),
-            jax.ShapeDtypeStruct((LAYERS, ROWS, LATENT), bf16),
-            jax.ShapeDtypeStruct((4, 2, 2 * HALF, T), bf16),
+            jax.ShapeDtypeStruct((3, ROWS, LATENT), bf16),
         ),
         in_specs=[hbm] * 3,
-        out_specs=(vmem,) * 4,
+        out_specs=(vmem,) * 3,
         scratch_shapes=[
             pltpu.VMEM((3, LAYERS, ROWS, LATENT), bf16),
             pltpu.VMEM((LAYERS, ROWS, LATENT), bf16),
+            pltpu.VMEM((LAYERS, ROWS, LATENT), bf16),
             pltpu.VMEM((LAYERS, 2, ROWS, ROWS), bf16),
+            pltpu.VMEM((2, 6 * CHUNK, LATENT), bf16),
             pltpu.VMEM((2, 6 * CHUNK, LATENT), bf16),
             pltpu.VMEM((2 * HALF, T), f32),
             pltpu.VMEM((HALF, T), f32),
             pltpu.VMEM((HALF, T), f32),
             pltpu.VMEM((15, PIECE, T), f32),
             pltpu.VMEM((2 * HALF, T), f32),
-            pltpu.VMEM((LATENT, LATENT), f32),
-            pltpu.VMEM((2, LATENT // 2, LATENT), bf16),
+            pltpu.VMEM((2, LATENT, LATENT), bf16),
             pltpu.SemaphoreType.REGULAR((3,)),
             dma((3, LAYERS)), dma((2, 6)), dma((2, 6)), dma, dma,
             dma((15,)), dma((15,)), dma((15,)), dma((15,)), dma((16,)), dma((16,)),
-            dma((3, 2, SHARES)), dma((3, 2, SHARES)), dma((3, 2, SHARES)), dma((3, 2, SHARES)),
-            dma, dma,
+            dma((2, 6)), dma((2, 6)),
         ],
         compiler_params=pltpu.CompilerParams(
             collective_id=0, has_side_effects=True, vmem_limit_bytes=32 << 20),
@@ -470,7 +426,7 @@
     return pl.pallas_call(
         finish,
         out_shape=(jax.ShapeDtypeStruct((LAYERS, ROWS, LATENT), f32),) * 2,
-        in_specs=[vmem] * 4,
+        in_specs=[vmem] * 3,
         out_specs=(hbm,) * 2,
         scratch_shapes=[pltpu.VMEM((3, ROWS, LATENT), f32), dma((LAYERS + 4,))],
         compiler_params=pltpu.CompilerParams(vmem_limit_bytes=12 << 20),

time: 55.5 us -> 54.2 us (0.977)
  Pallas kernels: 54.6 us -> 53.3 us
    pallas_call x1, Pallas kernels: 52.5 us -> 51.2 us  [shards(): pl.pallas_call(exchange, out_shape=(jax.ShapeDtypeStruct((LAYERS, ROWS, L...]
where the time goes in v7:
time: 54.2 us; the launch traced here: 54.1 us
  Pallas kernels  53.3 us (98%)
  between operations  0.8 us (1%)
    pallas_call x1, Pallas kernels, shards(): pl.pallas_call(exchange, out_shape=(jax.ShapeDtypeStruct((LAYERS, ROWS, L...  51.2 us
    pallas_call x1, Pallas kernels, shards(): pl.pallas_call(finish, out_shape=(jax.ShapeDtypeStruct((LAYERS, ROWS, LAT...  2.1 us

profile of v7, /device:TPU:1, one launch (start us, length us, event | category | flops | bytes accessed | tf_op | source)
XLA Modules:
  0.0 54.1 jit_solution(13233121238259084797)
XLA Ops:
  0.6 51.2 %exchange.1 = (f32[4,256,512]{2,1,0:T(8,128)S(1)}, f32[256,512]{1,0:T(8,128)S(1)}, bf16[3,256,512]{2,1,0:T(8,128)(2,1)S(1)}) custom-call(bf16[4,256,512]{2,1,0:T(8,128)(2,1)} %m_hbm.1, bf16[4,256,512]{2,1,0:T(8,128)(2,1)} %g1_hbm.1, bf16[4,256,512]{2,1,0:T(8,128)(2,1)} %g2_hbm.1), custom_call_target="tpu_custom_call" | custom-call | tf_op jit(solution)/shard_map/exchange/pallas_call | solution.py:392
  51.8 2.1 %finish.1 = (f32[4,256,512]{2,1,0:T(8,128)}, f32[4,256,512]{2,1,0:T(8,128)}) custom-call(f32[4,256,512]{2,1,0:T(8,128)S(1)} %get-tuple-element.5.o1_ref, f32[256,512]{1,0:T(8,128)S(1)} %get-tuple-element.6.own2_ref, bf16[3,256,512]{2,1,0:T(8,128)(2,1)S(1)} %get-tuple-element.7.got), custom_call_target="tpu_custom_call" | custom-call | tf_op jit(solution)/shard_map/finish/pallas_call | solution.py:426

commit v8 on v7

--- a/solution.py
+++ b/solution.py
@@ -25,9 +25,10 @@
 HALF = len(BLOCKS) * T // 2
 PIECE = HALF // 16
 CHUNK = 64
-OFFSETS = [(1, 1, 2), (1, 1, 0), (1, 0, 2), (0, 1, 2)]
-OFFSETS += [(i, j, z) for z in (1, 3) for i in (0, 1) for j in (0, 1)]
-OFFSETS += [(1, 0, 0), (0, 1, 0), (0, 0, 2)]
+OFFSETS = [(1, 1, 2), (1, 1, 0), (1, 0, 2)]
+OFFSETS += [(1, j, z) for z in (1, 3) for j in (0, 1)] + [(1, 0, 0)]
+OFFSETS += [(0, 1, 2)] + [(0, j, z) for z in (1, 3) for j in (0, 1)]
+OFFSETS += [(0, 1, 0), (0, 0, 2)]
 
 
 def split(x):
@@ -71,16 +72,19 @@
     return rows == lax.broadcasted_iota(jnp.int32, (n, n), 1)
 
 
-def layer_polynomial(gram):
+def layer_polynomial(gram, scratch, start):
+    n = gram.shape[0]
     diag = jnp.where(eye(gram.shape[0]), f32(quintic_a), f32(0.0))
     s, q = gram, None
     for k in range(NS_ITERS):
         part = split(s)
         m = diag + (quintic_b * s + quintic_c * square_even(part))
+        if k == 0:
+            scratch[...] = m
         ms = split(m)
         if k < NS_ITERS - 1:
             s = mm_even(split(mm_even(part, ms)), ms)
-        q = m if k == 0 else mm_even(split(q), ms)
+        q = scratch[pl.ds(start, n // 2), :] if k == 0 else dot3(split(q), ms)
     return q
 
 
@@ -118,9 +122,10 @@
 
 def exchange(
     m_hbm, g1_hbm, g2_hbm, o1_ref, own2_ref, got,
-    ins, y1_ref, y2_ref, q1_ref, rx, tx, part, core_in, own, rs, gath, q2_ref, rounds,
+    ins, y1_ref, y2_ref, q1_ref, rx, rx2, mate, tx, stage, part, core_in, own, rs, gath,
+    q_full, q2_ref, rounds,
     s_in, s_row, r_row, s_core, r_core, s_rs, r_rs, s_ag, r_ag, s_rel, r_rel,
-    s_q, r_q,
+    s_q, r_q, s_mate, r_mate, s_own, r_own,
 ):
     x = lax.axis_index("layer")
     head = lax.axis_index("head")
@@ -157,7 +162,7 @@
 
     barrier = pltpu.get_barrier_semaphore()
     greet = [partner]
-    greet += [at(*p, c) for p in steps]
+    greet += [at(*p, k) for p in steps for k in (c, 1 - c)]
     for who in greet:
         pl.semaphore_signal(barrier, inc=1, device_id=who, device_id_type=MESH)
 
@@ -204,20 +209,15 @@
             y1_ref[n] = one
             y2_ref[n] = (momentum_decay * one.astype(f32) + ins[2, w].astype(f32)).astype(bf16)
 
-        if w == 0:
-            @phase("w_tell")
-            def _():
-                pl.semaphore_wait(rounds.at[0], len(told[0]))
-                tell(1)
         if w < 3:
             for h in range(2):
                 for k in (2 * w, 2 * w + 1):
                     row_copies[h][k].start()
 
-    @phase("w_rounds")
-    def _():
-        pl.semaphore_wait(rounds.at[1], len(told[1]))
-        tell(2)
+    @phase("w_tell")
+    def _():
+        pl.semaphore_wait(rounds.at[0], len(told[0]))
+        tell(1)
 
     def heads(ns):
         grams = []
@@ -257,6 +257,8 @@
 
     @phase("w_rows1")
     def _():
+        pl.semaphore_wait(rounds.at[1], len(told[1]))
+        tell(2)
         for copy in row_copies[1]:
             copy.wait()
 
@@ -266,21 +268,36 @@
 
     theirs = pl.ds(pl.multiple_of((1 - c) * HALF, 8), HALF)
     mine = pl.ds(pl.multiple_of(c * HALF, 8), HALF)
-    swap = send(part.at[theirs, :], core_in, s_core, r_core, partner)
-    swap.start()
-    @phase("w_swap")
-    def _():
-        swap.wait()
-        own[...] = part[mine, :] + core_in[...]
-
+    def section(core, side):
+        return pl.ds(pl.multiple_of(core * HALF + side * (HALF // 2), 8), HALF // 2)
+
+    sides = [1 - i, i]
+    swaps = [
+        send(part.at[section(1 - c, side), :], core_in.at[section(0, side), :], s_core.at[k],
+             r_core.at[k], partner)
+        for k, side in enumerate(sides)
+    ]
     rs_copies = []
     for k, (p, t2) in enumerate(team):
         rs_copies.append(send(
             own.at[pl.ds(pl.multiple_of(t2 * PIECE, 8), PIECE), :], rs.at[k],
             s_rs.at[k], r_rs.at[k], at(*p, c)))
-    pl.semaphore_wait(rounds.at[2], len(told[2]))
-    for copy in rs_copies:
+    mates = [send(rx, rx2, s_mate.at[0], r_mate.at[0], partner),
+             send(y2_ref.at[lay], mate, s_mate.at[1], r_mate.at[1], partner)]
+    for copy in swaps:
         copy.start()
+
+    @phase("w_swap")
+    def _():
+        pl.semaphore_wait(rounds.at[2], len(told[2]))
+        for k, side in enumerate(sides):
+            swaps[k].wait()
+            own[section(0, side), :] = part[section(c, side), :] + core_in[section(0, side), :]
+            for copy in (rs_copies[:8] if k == 0 else rs_copies[8:]):
+                copy.start()
+        for copy in mates:
+            copy.start()
+
     @phase("p04")
     def _():
         heads((0, 1))
@@ -334,35 +351,60 @@
     def _():
         gram = unpacked(gath[...])
         norm = jnp.sqrt(trace(gram)) + norm_epsilon
-        q = layer_polynomial(gram * (1.0 / (norm * norm)))
-        q2_ref[0], q2_ref[1] = split(q * (math.sqrt(ALL_ROWS) / norm))
-
+        q = layer_polynomial(
+            gram * (1.0 / (norm * norm)), q_full, pl.multiple_of(c * 256, 256))
+        q2_ref[0], q2_ref[1] = split((q * (math.sqrt(ALL_ROWS) / norm)).T)
+
+    def columns(core):
+        return pl.ds(pl.multiple_of(core * 256, 256), 256)
+
+    def returned(h, k, d, core):
+        return send(
+            tx.at[h, d, pl.ds(k * CHUNK, CHUNK), :],
+            got.at[k // 2, pl.ds((k % 2) * 128 + h * CHUNK, CHUNK), columns(core)],
+            s_q.at[h, k, d], r_q.at[h, k, core], at(*steps[k ^ 1], c if d == 0 else 1 - c))
+
+    for copy in mates:
+        copy.wait()
     back = []
     for h in range(2):
         @phase("p07")
         def _(h=h):
-            w = rx[h]
-            tx[h] = (dot(w, q2_ref[0]) + dot(w, q2_ref[1])).astype(bf16)
-
-        for k, p in enumerate(steps):
-            back.append(send(
-                tx.at[h, pl.ds(k * CHUNK, CHUNK), :],
-                got.at[k // 2, pl.ds((k % 2) * 128 + h * CHUNK, CHUNK), :],
-                s_q.at[h, k], r_q.at[h, k], at(*steps[k ^ 1], c)))
-            back[-1].start()
+            for d, rows in enumerate((rx, rx2)):
+                w = rows[h]
+                tx[h, d] = (dot(w, q2_ref[0]) + dot(w, q2_ref[1])).astype(bf16)
+
+        for k in range(6):
+            for d in range(2):
+                back.append(returned(h, k, d, c))
+                back[-1].start()
 
     @phase("p08")
     def _():
+        w = mate[...]
+        stage[...] = dot(w, q2_ref[0]) + dot(w, q2_ref[1])
+
+    over = [send(stage, own2_ref.at[:, columns(k)], s_own, r_own, partner) for k in (c, 1 - c)]
+    over[0].start()
+
+    @phase("p09")
+    def _():
         w = y2_ref[lay]
-        own2_ref[...] = dot(w, q2_ref[0]) + dot(w, q2_ref[1])
+        own2_ref[:, columns(c)] = dot(w, q2_ref[0]) + dot(w, q2_ref[1])
         for n in range(LAYERS):
             v = y1_ref[n]
             o1_ref[n] = dot(q1_ref[n, 0], v) + dot(q1_ref[n, 1], v)
 
     @phase("w_back")
     def _():
+        over[0].wait_send()
+        over[1].wait_recv()
         for copy in back:
-            copy.wait()
+            copy.wait_send()
+        for h in range(2):
+            for k in range(6):
+                for core in range(2):
+                    returned(h, k, 0, core).wait_recv()
 
 
 def finish(o1_ref, own2_ref, got, out1, out2, buf, sems):
@@ -405,16 +447,20 @@
             pltpu.VMEM((LAYERS, 2, ROWS, ROWS), bf16),
             pltpu.VMEM((2, 6 * CHUNK, LATENT), bf16),
             pltpu.VMEM((2, 6 * CHUNK, LATENT), bf16),
+            pltpu.VMEM((ROWS, LATENT), bf16),
+            pltpu.VMEM((2, 2, 6 * CHUNK, LATENT // 2), bf16),
+            pltpu.VMEM((ROWS, LATENT // 2), f32),
             pltpu.VMEM((2 * HALF, T), f32),
             pltpu.VMEM((HALF, T), f32),
             pltpu.VMEM((HALF, T), f32),
             pltpu.VMEM((15, PIECE, T), f32),
             pltpu.VMEM((2 * HALF, T), f32),
-            pltpu.VMEM((2, LATENT, LATENT), bf16),
+            pltpu.VMEM((LATENT, LATENT), f32),
+            pltpu.VMEM((2, LATENT, LATENT // 2), bf16),
             pltpu.SemaphoreType.REGULAR((3,)),
-            dma((3, LAYERS)), dma((2, 6)), dma((2, 6)), dma, dma,
+            dma((3, LAYERS)), dma((2, 6)), dma((2, 6)), dma((2,)), dma((2,)),
             dma((15,)), dma((15,)), dma((15,)), dma((15,)), dma((16,)), dma((16,)),
-            dma((2, 6)), dma((2, 6)),
+            dma((2, 6, 2)), dma((2, 6, 2)), dma((2,)), dma((2,)), dma, dma,
         ],
         compiler_params=pltpu.CompilerParams(
             collective_id=0, has_side_effects=True, vmem_limit_bytes=32 << 20),

time: 54.2 us -> 53.4 us (0.985)
  Pallas kernels: 53.3 us -> 52.5 us
    pallas_call x1, Pallas kernels: 51.2 us -> 50.4 us  [shards(): pl.pallas_call(exchange, out_shape=(jax.ShapeDtypeStruct((LAYERS, ROWS, L...]
where the time goes in v8:
time: 53.4 us; the launch traced here: 53.3 us
  Pallas kernels  52.5 us (98%)
  between operations  0.8 us (1%)
    pallas_call x1, Pallas kernels, shards(): pl.pallas_call(exchange, out_shape=(jax.ShapeDtypeStruct((LAYERS, ROWS, L...  50.4 us
    pallas_call x1, Pallas kernels, shards(): pl.pallas_call(finish, out_shape=(jax.ShapeDtypeStruct((LAYERS, ROWS, LAT...  2.1 us

profile of v8, /device:TPU:1, one launch (start us, length us, event | category | flops | bytes accessed | tf_op | source)
XLA Modules:
  0.0 53.3 jit_solution(10180536209540017537)
XLA Ops:
  0.6 50.4 %exchange.1 = (f32[4,256,512]{2,1,0:T(8,128)S(1)}, f32[256,512]{1,0:T(8,128)S(1)}, bf16[3,256,512]{2,1,0:T(8,128)(2,1)S(1)}) custom-call(bf16[4,256,512]{2,1,0:T(8,128)(2,1)} %m_hbm.1, bf16[4,256,512]{2,1,0:T(8,128)(2,1)} %g1_hbm.1, bf16[4,256,512]{2,1,0:T(8,128)(2,1)} %g2_hbm.1), custom_call_target="tpu_custom_call" | custom-call | tf_op jit(solution)/shard_map/exchange/pallas_call | solution.py:434
  51.1 2.1 %finish.1 = (f32[4,256,512]{2,1,0:T(8,128)}, f32[4,256,512]{2,1,0:T(8,128)}) custom-call(f32[4,256,512]{2,1,0:T(8,128)S(1)} %get-tuple-element.5.o1_ref, f32[256,512]{1,0:T(8,128)S(1)} %get-tuple-element.6.own2_ref, bf16[3,256,512]{2,1,0:T(8,128)(2,1)S(1)} %get-tuple-element.7.got), custom_call_target="tpu_custom_call" | custom-call | tf_op jit(solution)/shard_map/finish/pallas_call | solution.py:472

commit v9 on v8

--- a/solution.py
+++ b/solution.py
@@ -29,6 +29,7 @@
 OFFSETS += [(1, j, z) for z in (1, 3) for j in (0, 1)] + [(1, 0, 0)]
 OFFSETS += [(0, 1, 2)] + [(0, j, z) for z in (1, 3) for j in (0, 1)]
 OFFSETS += [(0, 1, 0), (0, 0, 2)]
+FAR = [0, 1, 2, 8]
 
 
 def split(x):
@@ -160,19 +161,21 @@
         return run
 
 
+    turn = lays + [lay]
+    loads = [
+        [pltpu.make_async_copy(h.at[n], ins.at[k, w], s_in.at[w])
+         for k, h in enumerate((m_hbm, g1_hbm, g2_hbm))]
+        for w, n in enumerate(turn)
+    ]
+    for copy in loads[0]:
+        copy.start()
     barrier = pltpu.get_barrier_semaphore()
     greet = [partner]
     greet += [at(*p, k) for p in steps for k in (c, 1 - c)]
     for who in greet:
         pl.semaphore_signal(barrier, inc=1, device_id=who, device_id_type=MESH)
 
-    turn = lays + [lay]
-    loads = [
-        [pltpu.make_async_copy(h.at[n], ins.at[k, w], s_in.at[k, w])
-         for k, h in enumerate((m_hbm, g1_hbm, g2_hbm))]
-        for w, n in enumerate(turn)
-    ]
-    for group in loads:
+    for group in loads[1:]:
         for copy in group:
             copy.start()
     def send(src, dst, ss, rr, who):
@@ -182,7 +185,7 @@
 
     row_copies = [
         [send(y2_ref.at[lays[k // 2], pl.ds((k % 2) * 128 + h * CHUNK, CHUNK), :],
-              rx.at[h, pl.ds(k * CHUNK, CHUNK), :], s_row.at[h, k], r_row.at[h, k], at(*p, c))
+              rx.at[h, pl.ds(k * CHUNK, CHUNK), :], s_row.at[h], r_row.at[h], at(*p, c))
          for k, p in enumerate(steps)]
         for h in range(2)
     ]
@@ -200,19 +203,33 @@
         pl.semaphore_wait(barrier, len(greet))
         tell(0)
 
-    for w, n in enumerate(turn):
-        @phase("p01")
-        def _(w=w, n=n):
-            for copy in loads[w]:
-                copy.wait()
-            one = (momentum_decay * ins[0, w].astype(f32) + ins[1, w].astype(f32)).astype(bf16)
-            y1_ref[n] = one
-            y2_ref[n] = (momentum_decay * one.astype(f32) + ins[2, w].astype(f32)).astype(bf16)
-
-        if w < 3:
-            for h in range(2):
-                for k in (2 * w, 2 * w + 1):
-                    row_copies[h][k].start()
+    def loaded(w):
+        pltpu.make_async_copy(ins.at[:, w], ins.at[:, w], s_in.at[w]).wait()
+
+    def momentum(w, n, starts, rows):
+        for first in starts:
+            r = pl.ds(first, rows)
+            one = momentum_decay * ins[0, w, r, :].astype(f32) + ins[1, w, r, :].astype(f32)
+            one = one.astype(bf16)
+            y1_ref[n, r, :] = one
+            two = momentum_decay * one.astype(f32) + ins[2, w, r, :].astype(f32)
+            y2_ref[n, r, :] = two.astype(bf16)
+
+    for h in range(2):
+        for w in range(3):
+            @phase("p01")
+            def _(h=h, w=w):
+                if h == 0:
+                    loaded(w)
+                momentum(w, turn[w], (h * CHUNK, 128 + h * CHUNK), CHUNK)
+
+            for k in (2 * w, 2 * w + 1):
+                row_copies[h][k].start()
+
+    @phase("p01o")
+    def _():
+        loaded(3)
+        momentum(3, lay, (0,), ROWS)
 
     @phase("w_tell")
     def _():
@@ -246,21 +263,23 @@
                 value = total[:, (j4 - i4) * T:(j4 - i4 + 1) * T]
                 part[rows, :] = value if first else part[rows, :] + value
 
+    @phase("p_own")
+    def _():
+        gram_of([y2_ref.at[lay]], True)
+
     @phase("w_rows0")
     def _():
-        for copy in row_copies[0]:
-            copy.wait()
+        send(rx.at[0], rx.at[0], s_row.at[0], r_row.at[0], partner).wait()
 
     @phase("p02")
     def _():
-        gram_of([y2_ref.at[lay], rx.at[0]], True)
+        gram_of([rx.at[0]], False)
 
     @phase("w_rows1")
     def _():
         pl.semaphore_wait(rounds.at[1], len(told[1]))
         tell(2)
-        for copy in row_copies[1]:
-            copy.wait()
+        send(rx.at[1], rx.at[1], s_row.at[1], r_row.at[1], partner).wait()
 
     @phase("p03")
     def _():
@@ -281,7 +300,7 @@
     for k, (p, t2) in enumerate(team):
         rs_copies.append(send(
             own.at[pl.ds(pl.multiple_of(t2 * PIECE, 8), PIECE), :], rs.at[k],
-            s_rs.at[k], r_rs.at[k], at(*p, c)))
+            s_rs, r_rs, at(*p, c)))
     mates = [send(rx, rx2, s_mate.at[0], r_mate.at[0], partner),
              send(y2_ref.at[lay], mate, s_mate.at[1], r_mate.at[1], partner)]
     for copy in swaps:
@@ -304,8 +323,7 @@
 
     @phase("w_rs")
     def _():
-        for copy in rs_copies:
-            copy.wait()
+        send(rs, rs, s_rs, r_rs, partner).wait()
 
     total = own[pl.ds(pl.multiple_of(t * PIECE, 8), PIECE), :]
     for k in range(15):
@@ -313,44 +331,44 @@
     here = pl.ds(pl.multiple_of(c * HALF + t * PIECE, 8), PIECE)
     gath[here, :] = total
     ag_copies = [
-        send(gath.at[here, :], gath.at[here, :], s_ag.at[k], r_ag.at[k], at(*p, c))
+        send(gath.at[here, :], gath.at[here, :], s_ag, r_ag.at[int(k in FAR)], at(*p, c))
         for k, (p, _) in enumerate(team)
     ]
     for copy in ag_copies:
         copy.start()
+
     @phase("p05")
     def _():
         heads((2, 3))
 
     def relay(k, t3, core):
         there = pl.ds(pl.multiple_of(core * HALF + t3 * PIECE, 8), PIECE)
-        return send(gath.at[there, :], gath.at[there, :], s_rel.at[k], r_rel.at[k], partner)
+        return send(gath.at[there, :], gath.at[there, :], s_rel, r_rel, partner)
 
     relays = [(15, t)]
     for k, (di, dj, dz) in enumerate(OFFSETS):
         relays.append((k, (((i + di) % 2) * 2 + (j + dj) % 2) * 4 + (z + 4 - dz) % 4))
     @phase("w_ag")
     def _():
-        for k, t3 in [relays[0]] + relays[:0:-1]:
-            if k < 15:
-                there = pl.ds(pl.multiple_of(c * HALF + t3 * PIECE, 8), PIECE)
-                send(gath.at[there, :], gath.at[there, :], s_ag.at[k], r_ag.at[k],
-                     at(*team[k][0], c)).wait_recv()
-            relay(k, t3, c).start()
+        relay(*relays[0], c).start()
+        for group in range(2):
+            ks = [k for k in range(15) if (k in FAR) == (group == 1)]
+            some = rs.at[pl.ds(0, len(ks))]
+            send(some, some, s_ag, r_ag.at[group], partner).wait_recv()
+            for k in ks:
+                relay(*relays[k + 1], c).start()
 
     @phase("w_relay")
     def _():
-        for copy in ag_copies:
-            copy.wait_send()
-        for k, t3 in relays:
-            relay(k, t3, c).wait_send()
-        for k, t3 in relays:
-            relay(k, t3, 1 - c).wait_recv()
+        send(rs, rs, s_ag, r_ag.at[0], partner).wait_send()
+        send(gath.at[mine, :], gath.at[mine, :], s_rel, r_rel, partner).wait_send()
+        send(gath.at[theirs, :], gath.at[theirs, :], s_rel, r_rel, partner).wait_recv()
 
     @phase("p06")
     def _():
         gram = unpacked(gath[...])
-        norm = jnp.sqrt(trace(gram)) + norm_epsilon
+        norm = jnp.sqrt(sum(trace(gram[k:k + T, k:k + T]) for k in range(0, LATENT, T)))
+        norm = norm + norm_epsilon
         q = layer_polynomial(
             gram * (1.0 / (norm * norm)), q_full, pl.multiple_of(c * 256, 256))
         q2_ref[0], q2_ref[1] = split((q * (math.sqrt(ALL_ROWS) / norm)).T)
@@ -362,7 +380,7 @@
         return send(
             tx.at[h, d, pl.ds(k * CHUNK, CHUNK), :],
             got.at[k // 2, pl.ds((k % 2) * 128 + h * CHUNK, CHUNK), columns(core)],
-            s_q.at[h, k, d], r_q.at[h, k, core], at(*steps[k ^ 1], c if d == 0 else 1 - c))
+            s_q, r_q, at(*steps[k ^ 1], c if d == 0 else 1 - c))
 
     for copy in mates:
         copy.wait()
@@ -399,12 +417,7 @@
     def _():
         over[0].wait_send()
         over[1].wait_recv()
-        for copy in back:
-            copy.wait_send()
-        for h in range(2):
-            for k in range(6):
-                for core in range(2):
-                    returned(h, k, 0, core).wait_recv()
+        send(got, got, s_q, r_q, partner).wait()
 
 
 def finish(o1_ref, own2_ref, got, out1, out2, buf, sems):
@@ -458,9 +471,8 @@
             pltpu.VMEM((LATENT, LATENT), f32),
             pltpu.VMEM((2, LATENT, LATENT // 2), bf16),
             pltpu.SemaphoreType.REGULAR((3,)),
-            dma((3, LAYERS)), dma((2, 6)), dma((2, 6)), dma((2,)), dma((2,)),
-            dma((15,)), dma((15,)), dma((15,)), dma((15,)), dma((16,)), dma((16,)),
-            dma((2, 6, 2)), dma((2, 6, 2)), dma((2,)), dma((2,)), dma, dma,
+            dma((LAYERS,)), dma((2,)), dma((2,)), dma((2,)), dma((2,)),
+            dma, dma, dma, dma((2,)), dma, dma, dma, dma, dma((2,)), dma((2,)), dma, dma,
         ],
         compiler_params=pltpu.CompilerParams(
             collective_id=0, has_side_effects=True, vmem_limit_bytes=32 << 20),

time: 53.4 us -> 52 us (0.974)
  Pallas kernels: 52.5 us -> 51 us
    pallas_call x1, Pallas kernels: 50.4 us -> 48.9 us  [shards(): pl.pallas_call(exchange, out_shape=(jax.ShapeDtypeStruct((LAYERS, ROWS, L...]
where the time goes in v9:
time: 52 us; the launch traced here: 51.8 us
  Pallas kernels  51 us (98%)
  between operations  0.8 us (2%)
    pallas_call x1, Pallas kernels, shards(): pl.pallas_call(exchange, out_shape=(jax.ShapeDtypeStruct((LAYERS, ROWS, L...  48.9 us
    pallas_call x1, Pallas kernels, shards(): pl.pallas_call(finish, out_shape=(jax.ShapeDtypeStruct((LAYERS, ROWS, LAT...  2.1 us

profile of v9, /device:TPU:1, one launch (start us, length us, event | category | flops | bytes accessed | tf_op | source)
XLA Modules:
  0.0 51.8 jit_solution(15817482125191422060)
XLA Ops:
  0.6 48.9 %exchange.1 = (f32[4,256,512]{2,1,0:T(8,128)S(1)}, f32[256,512]{1,0:T(8,128)S(1)}, bf16[3,256,512]{2,1,0:T(8,128)(2,1)S(1)}) custom-call(bf16[4,256,512]{2,1,0:T(8,128)(2,1)} %m_hbm.1, bf16[4,256,512]{2,1,0:T(8,128)(2,1)} %g1_hbm.1, bf16[4,256,512]{2,1,0:T(8,128)(2,1)} %g2_hbm.1), custom_call_target="tpu_custom_call" | custom-call | tf_op jit(solution)/shard_map/exchange/pallas_call | solution.py:447
  49.6 2.1 %finish.1 = (f32[4,256,512]{2,1,0:T(8,128)}, f32[4,256,512]{2,1,0:T(8,128)}) custom-call(f32[4,256,512]{2,1,0:T(8,128)S(1)} %get-tuple-element.5.o1_ref, f32[256,512]{1,0:T(8,128)S(1)} %get-tuple-element.6.own2_ref, bf16[3,256,512]{2,1,0:T(8,128)(2,1)S(1)} %get-tuple-element.7.got), custom_call_target="tpu_custom_call" | custom-call | tf_op jit(solution)/shard_map/finish/pallas_call | solution.py:484

commit v10 on v9

--- a/solution.py
+++ b/solution.py
@@ -23,7 +23,7 @@
 T = 128
 BLOCKS = [(i, j) for i in range(4) for j in range(i, 4)]
 HALF = len(BLOCKS) * T // 2
-PIECE = HALF // 16
+PIECE = HALF // 8
 CHUNK = 64
 OFFSETS = [(1, 1, 2), (1, 1, 0), (1, 0, 2)]
 OFFSETS += [(1, j, z) for z in (1, 3) for j in (0, 1)] + [(1, 0, 0)]
@@ -123,9 +123,9 @@
 
 def exchange(
     m_hbm, g1_hbm, g2_hbm, o1_ref, own2_ref, got,
-    ins, y1_ref, y2_ref, q1_ref, rx, rx2, mate, tx, stage, part, core_in, own, rs, gath,
+    ins, y1_ref, y2_ref, q1_ref, rx, mate, tx, stage, part, rs, gath,
     q_full, q2_ref, rounds,
-    s_in, s_row, r_row, s_core, r_core, s_rs, r_rs, s_ag, r_ag, s_rel, r_rel,
+    s_in, s_row, r_row, s_rs, r_rs, s_ag, r_ag, s_rel, r_rel,
     s_q, r_q, s_mate, r_mate, s_own, r_own,
 ):
     x = lax.axis_index("layer")
@@ -154,10 +154,10 @@
     partner = at(x, y, z, 1 - c)
     always = x < 4
 
-    def phase(name):
+    def phase(name, lead=False):
         def run(body):
             with jax.named_scope(name):
-                pl.when(always)(body)
+                pl.when(c == 1 if lead else always)(body)
         return run
 
 
@@ -185,11 +185,13 @@
 
     row_copies = [
         [send(y2_ref.at[lays[k // 2], pl.ds((k % 2) * 128 + h * CHUNK, CHUNK), :],
-              rx.at[h, pl.ds(k * CHUNK, CHUNK), :], s_row.at[h], r_row.at[h], at(*p, c))
+              rx.at[h, pl.ds(pl.multiple_of((k * 2 + c) * CHUNK, CHUNK), CHUNK), :],
+              s_row.at[h], r_row.at[h], at(*p, 1))
          for k, p in enumerate(steps)]
         for h in range(2)
     ]
-
+    mates = [send(y2_ref.at[lay], mate, s_mate.at[0], r_mate.at[0], partner),
+             send(rx, rx, s_mate.at[1], r_mate.at[1], partner)]
     near = [at(*p, c) for p in steps]
     far = [at((x + 2) % 4, y, z, c), at(x, (y + 2) % 4, z, c), at(x, y, (z + 2) % 4, c)]
     told = [near, near + far, far[:1]]
@@ -230,6 +232,8 @@
     def _():
         loaded(3)
         momentum(3, lay, (0,), ROWS)
+
+    mates[0].start()
 
     @phase("w_tell")
     def _():
@@ -263,15 +267,23 @@
                 value = total[:, (j4 - i4) * T:(j4 - i4 + 1) * T]
                 part[rows, :] = value if first else part[rows, :] + value
 
-    @phase("p_own")
-    def _():
-        gram_of([y2_ref.at[lay]], True)
+    mates[0].wait()
+
+    @phase("p_own", True)
+    def _():
+        gram_of([y2_ref.at[lay], mate], True)
 
     @phase("w_rows0")
     def _():
-        send(rx.at[0], rx.at[0], s_row.at[0], r_row.at[0], partner).wait()
-
-    @phase("p02")
+        for h in range(2):
+            sent = rx.at[h, pl.ds(0, 6 * CHUNK), :]
+            send(sent, sent, s_row.at[h], r_row.at[h], partner).wait_send()
+
+    @phase("w_rows", True)
+    def _():
+        send(rx.at[0], rx.at[0], s_row.at[0], r_row.at[0], partner).wait_recv()
+
+    @phase("p02", True)
     def _():
         gram_of([rx.at[0]], False)
 
@@ -279,90 +291,76 @@
     def _():
         pl.semaphore_wait(rounds.at[1], len(told[1]))
         tell(2)
-        send(rx.at[1], rx.at[1], s_row.at[1], r_row.at[1], partner).wait()
-
-    @phase("p03")
+
+    @phase("w_rows1b", True)
+    def _():
+        send(rx.at[1], rx.at[1], s_row.at[1], r_row.at[1], partner).wait_recv()
+
+    @phase("p03", True)
     def _():
         gram_of([rx.at[1]], False)
 
-    theirs = pl.ds(pl.multiple_of((1 - c) * HALF, 8), HALF)
-    mine = pl.ds(pl.multiple_of(c * HALF, 8), HALF)
-    def section(core, side):
-        return pl.ds(pl.multiple_of(core * HALF + side * (HALF // 2), 8), HALF // 2)
-
-    sides = [1 - i, i]
-    swaps = [
-        send(part.at[section(1 - c, side), :], core_in.at[section(0, side), :], s_core.at[k],
-             r_core.at[k], partner)
-        for k, side in enumerate(sides)
-    ]
     rs_copies = []
     for k, (p, t2) in enumerate(team):
         rs_copies.append(send(
-            own.at[pl.ds(pl.multiple_of(t2 * PIECE, 8), PIECE), :], rs.at[k],
-            s_rs, r_rs, at(*p, c)))
-    mates = [send(rx, rx2, s_mate.at[0], r_mate.at[0], partner),
-             send(y2_ref.at[lay], mate, s_mate.at[1], r_mate.at[1], partner)]
-    for copy in swaps:
-        copy.start()
-
-    @phase("w_swap")
-    def _():
-        pl.semaphore_wait(rounds.at[2], len(told[2]))
-        for k, side in enumerate(sides):
-            swaps[k].wait()
-            own[section(0, side), :] = part[section(c, side), :] + core_in[section(0, side), :]
-            for copy in (rs_copies[:8] if k == 0 else rs_copies[8:]):
-                copy.start()
-        for copy in mates:
+            part.at[pl.ds(pl.multiple_of(t2 * PIECE, 8), PIECE), :], rs.at[k],
+            s_rs, r_rs, at(*p, 1)))
+
+    pl.semaphore_wait(rounds.at[2], len(told[2]))
+
+    @phase("s_rs", True)
+    def _():
+        for copy in rs_copies:
             copy.start()
+        mates[1].start()
 
     @phase("p04")
     def _():
         heads((0, 1))
 
-    @phase("w_rs")
-    def _():
-        send(rs, rs, s_rs, r_rs, partner).wait()
-
-    total = own[pl.ds(pl.multiple_of(t * PIECE, 8), PIECE), :]
-    for k in range(15):
-        total = total + rs[k]
-    here = pl.ds(pl.multiple_of(c * HALF + t * PIECE, 8), PIECE)
-    gath[here, :] = total
+    here = pl.ds(pl.multiple_of(t * PIECE, 8), PIECE)
     ag_copies = [
-        send(gath.at[here, :], gath.at[here, :], s_ag, r_ag.at[int(k in FAR)], at(*p, c))
+        send(gath.at[here, :], gath.at[here, :], s_ag, r_ag.at[int(k in FAR)], at(*p, 1))
         for k, (p, _) in enumerate(team)
     ]
-    for copy in ag_copies:
-        copy.start()
+
+    @phase("w_rs", True)
+    def _():
+        send(rs, rs, s_rs, r_rs, partner).wait()
+        total = part[here, :]
+        for k in range(15):
+            total = total + rs[k]
+        gath[here, :] = total
+
+    @phase("s_ag", True)
+    def _():
+        for copy in ag_copies:
+            copy.start()
 
     @phase("p05")
     def _():
         heads((2, 3))
 
-    def relay(k, t3, core):
-        there = pl.ds(pl.multiple_of(core * HALF + t3 * PIECE, 8), PIECE)
+    def relay(k, t3):
+        there = pl.ds(pl.multiple_of(t3 * PIECE, 8), PIECE)
         return send(gath.at[there, :], gath.at[there, :], s_rel, r_rel, partner)
 
     relays = [(15, t)]
     for k, (di, dj, dz) in enumerate(OFFSETS):
         relays.append((k, (((i + di) % 2) * 2 + (j + dj) % 2) * 4 + (z + 4 - dz) % 4))
-    @phase("w_ag")
-    def _():
-        relay(*relays[0], c).start()
+    @phase("w_ag", True)
+    def _():
+        relay(*relays[0]).start()
         for group in range(2):
             ks = [k for k in range(15) if (k in FAR) == (group == 1)]
             some = rs.at[pl.ds(0, len(ks))]
             send(some, some, s_ag, r_ag.at[group], partner).wait_recv()
             for k in ks:
-                relay(*relays[k + 1], c).start()
-
-    @phase("w_relay")
-    def _():
-        send(rs, rs, s_ag, r_ag.at[0], partner).wait_send()
-        send(gath.at[mine, :], gath.at[mine, :], s_rel, r_rel, partner).wait_send()
-        send(gath.at[theirs, :], gath.at[theirs, :], s_rel, r_rel, partner).wait_recv()
+                relay(*relays[k + 1]).start()
+
+    @pl.when(c == 0)
+    def _():
+        send(gath, gath, s_rel, r_rel, partner).wait_recv()
 
     @phase("p06")
     def _():
@@ -378,19 +376,20 @@
 
     def returned(h, k, d, core):
         return send(
-            tx.at[h, d, pl.ds(k * CHUNK, CHUNK), :],
+            tx.at[h, pl.ds((k * 2 + d) * CHUNK, CHUNK), :],
             got.at[k // 2, pl.ds((k % 2) * 128 + h * CHUNK, CHUNK), columns(core)],
-            s_q, r_q, at(*steps[k ^ 1], c if d == 0 else 1 - c))
-
-    for copy in mates:
-        copy.wait()
+            s_q, r_q, at(*steps[k ^ 1], d))
+
+    @pl.when(c == 0)
+    def _():
+        mates[1].wait_recv()
+
     back = []
     for h in range(2):
         @phase("p07")
         def _(h=h):
-            for d, rows in enumerate((rx, rx2)):
-                w = rows[h]
-                tx[h, d] = (dot(w, q2_ref[0]) + dot(w, q2_ref[1])).astype(bf16)
+            w = rx[h]
+            tx[h] = (dot(w, q2_ref[0]) + dot(w, q2_ref[1])).astype(bf16)
 
         for k in range(6):
             for d in range(2):
@@ -412,6 +411,12 @@
         for n in range(LAYERS):
             v = y1_ref[n]
             o1_ref[n] = dot(q1_ref[n, 0], v) + dot(q1_ref[n, 1], v)
+
+    @phase("w_sent", True)
+    def _():
+        mates[1].wait_send()
+        send(rs, rs, s_ag, r_ag.at[0], partner).wait_send()
+        send(gath, gath, s_rel, r_rel, partner).wait_send()
 
     @phase("w_back")
     def _():
@@ -458,20 +463,17 @@
             pltpu.VMEM((LAYERS, ROWS, LATENT), bf16),
             pltpu.VMEM((LAYERS, ROWS, LATENT), bf16),
             pltpu.VMEM((LAYERS, 2, ROWS, ROWS), bf16),
-            pltpu.VMEM((2, 6 * CHUNK, LATENT), bf16),
-            pltpu.VMEM((2, 6 * CHUNK, LATENT), bf16),
+            pltpu.VMEM((2, 12 * CHUNK, LATENT), bf16),
             pltpu.VMEM((ROWS, LATENT), bf16),
-            pltpu.VMEM((2, 2, 6 * CHUNK, LATENT // 2), bf16),
+            pltpu.VMEM((2, 12 * CHUNK, LATENT // 2), bf16),
             pltpu.VMEM((ROWS, LATENT // 2), f32),
             pltpu.VMEM((2 * HALF, T), f32),
-            pltpu.VMEM((HALF, T), f32),
-            pltpu.VMEM((HALF, T), f32),
             pltpu.VMEM((15, PIECE, T), f32),
             pltpu.VMEM((2 * HALF, T), f32),
             pltpu.VMEM((LATENT, LATENT), f32),
             pltpu.VMEM((2, LATENT, LATENT // 2), bf16),
             pltpu.SemaphoreType.REGULAR((3,)),
-            dma((LAYERS,)), dma((2,)), dma((2,)), dma((2,)), dma((2,)),
+            dma((LAYERS,)), dma((2,)), dma((2,)),
             dma, dma, dma, dma((2,)), dma, dma, dma, dma, dma((2,)), dma((2,)), dma, dma,
         ],
         compiler_params=pltpu.CompilerParams(

time: 52 us -> 49.7 us (0.956)
  Pallas kernels: 51 us -> 48.8 us
    pallas_call x1, Pallas kernels: 48.9 us -> 46.7 us  [shards(): pl.pallas_call(exchange, out_shape=(jax.ShapeDtypeStruct((LAYERS, ROWS, L...]
where the time goes in v10:
time: 49.7 us; the launch traced here: 49.6 us
  Pallas kernels  48.8 us (98%)
  between operations  0.8 us (2%)
    pallas_call x1, Pallas kernels, shards(): pl.pallas_call(exchange, out_shape=(jax.ShapeDtypeStruct((LAYERS, ROWS, L...  46.7 us
    pallas_call x1, Pallas kernels, shards(): pl.pallas_call(finish, out_shape=(jax.ShapeDtypeStruct((LAYERS, ROWS, LAT...  2.1 us

profile of v10, /device:TPU:1, one launch (start us, length us, event | category | flops | bytes accessed | tf_op | source)
XLA Modules:
  0.0 49.6 jit_solution(15213780169301151406)
XLA Ops:
  0.6 46.7 %exchange.1 = (f32[4,256,512]{2,1,0:T(8,128)S(1)}, f32[256,512]{1,0:T(8,128)S(1)}, bf16[3,256,512]{2,1,0:T(8,128)(2,1)S(1)}) custom-call(bf16[4,256,512]{2,1,0:T(8,128)(2,1)} %m_hbm.1, bf16[4,256,512]{2,1,0:T(8,128)(2,1)} %g1_hbm.1, bf16[4,256,512]{2,1,0:T(8,128)(2,1)} %g2_hbm.1), custom_call_target="tpu_custom_call" | custom-call | tf_op jit(solution)/shard_map/exchange/pallas_call | solution.py:452
  47.3 2.1 %finish.1 = (f32[4,256,512]{2,1,0:T(8,128)}, f32[4,256,512]{2,1,0:T(8,128)}) custom-call(f32[4,256,512]{2,1,0:T(8,128)S(1)} %get-tuple-element.5.o1_ref, f32[256,512]{1,0:T(8,128)S(1)} %get-tuple-element.6.own2_ref, bf16[3,256,512]{2,1,0:T(8,128)(2,1)S(1)} %get-tuple-element.7.got), custom_call_target="tpu_custom_call" | custom-call | tf_op jit(solution)/shard_map/finish/pallas_call | solution.py:486

commit v11 on v10

--- a/solution.py
+++ b/solution.py
@@ -312,7 +312,6 @@
     def _():
         for copy in rs_copies:
             copy.start()
-        mates[1].start()
 
     @phase("p04")
     def _():
@@ -334,8 +333,9 @@
 
     @phase("s_ag", True)
     def _():
-        for copy in ag_copies:
-            copy.start()
+        for k in FAR + [k for k in range(15) if k not in FAR]:
+            ag_copies[k].start()
+        mates[1].start()
 
     @phase("p05")
     def _():

time: 49.7 us -> 49.7 us (level)
  no operation moved by 1% of the time
where the time goes in v11:
time: 49.7 us; the launch traced here: 49.6 us
  Pallas kernels  48.8 us (98%)
  between operations  0.8 us (2%)
    pallas_call x1, Pallas kernels, shards(): pl.pallas_call(exchange, out_shape=(jax.ShapeDtypeStruct((LAYERS, ROWS, L...  46.7 us
    pallas_call x1, Pallas kernels, shards(): pl.pallas_call(finish, out_shape=(jax.ShapeDtypeStruct((LAYERS, ROWS, LAT...  2.1 us

profile of v11, /device:TPU:1, one launch (start us, length us, event | category | flops | bytes accessed | tf_op | source)
XLA Modules:
  0.0 49.6 jit_solution(13235549490509883998)
XLA Ops:
  0.6 46.7 %exchange.1 = (f32[4,256,512]{2,1,0:T(8,128)S(1)}, f32[256,512]{1,0:T(8,128)S(1)}, bf16[3,256,512]{2,1,0:T(8,128)(2,1)S(1)}) custom-call(bf16[4,256,512]{2,1,0:T(8,128)(2,1)} %m_hbm.1, bf16[4,256,512]{2,1,0:T(8,128)(2,1)} %g1_hbm.1, bf16[4,256,512]{2,1,0:T(8,128)(2,1)} %g2_hbm.1), custom_call_target="tpu_custom_call" | custom-call | tf_op jit(solution)/shard_map/exchange/pallas_call | solution.py:452
  47.4 2.1 %finish.1 = (f32[4,256,512]{2,1,0:T(8,128)}, f32[4,256,512]{2,1,0:T(8,128)}) custom-call(f32[4,256,512]{2,1,0:T(8,128)S(1)} %get-tuple-element.5.o1_ref, f32[256,512]{1,0:T(8,128)S(1)} %get-tuple-element.6.own2_ref, bf16[3,256,512]{2,1,0:T(8,128)(2,1)S(1)} %get-tuple-element.7.got), custom_call_target="tpu_custom_call" | custom-call | tf_op jit(solution)/shard_map/finish/pallas_call | solution.py:486
